TPU v7x, 256 devices: a whole 4x4x8 slice. The times are simulated.
256 devices in a mesh: tm: 16 (over y, x_hi, core), col: 16 (over z, x_lo).
Axes of the slice: x: 4 (x_hi: 2, x_lo: 2; x = x_hi * 2 + x_lo), y: 4, z: 8, core: 2. Of those that a mesh axis runs over, the one named last changes fastest.
Arguments:
- occ_rows: bfloat16 [1024, 1024], P(None, 'col'), may hold values from -2.5 to 2.5
- emp_rows: bfloat16 [1024, 1024], P(None, 'col'), may hold values from -2.5 to 2.5
- occ_cols: bfloat16 [1024, 16384], P(None, 'col'), may hold values from -2.5 to 2.5
- emp_cols: bfloat16 [1024, 16384], P(None, 'col'), may hold values from -2.5 to 2.5
- occ_energy: float32 [1024], replicated, may hold values from 0.1 to 1.5
- emp_energy: float32 [1024], replicated, may hold values from 0.1 to 1.5
- time_points: float32 [16], replicated, may hold values from 0.1 to 2
- time_weights: float32 [16], replicated, may hold values from 0.1 to 1
- frequencies: float32 [16], replicated, may hold values from 0.1 to 4
- trial_vectors: float32 [16384, 512], P('col'), may hold values from -0.046875 to 0.046875
Outputs:
- response: float32 [16, 1024, 512], P('tm', 'col')
All inputs are finite; a program needn't handle non-finite values.
Results may differ from a plain program's by a relative error of at most 0.0025.
Values may be sent and summed in bfloat16 or wider, within the bound.
No kernel may reach another device: no remote copies, remote signals or barrier semaphores. Data moves between devices by JAX's collectives and lax.ppermute only.
A program may use at most 64 MiB of HBM per device.

v0:
```python
import jax
import jax.numpy as jnp
from jax import lax
from jax.sharding import Mesh
from jax.sharding import PartitionSpec as P

COL = ("col_0", "col_1")


def gathered_by_axis(value, axes, dim):
    for axis in reversed(axes):
        value = lax.all_gather(value, axis, axis=dim, tiled=True)
    return value


def split_up(value, dim, peers):
    lengths = value.shape
    parts = value.reshape(*lengths[:dim], peers, lengths[dim] // peers, *lengths[dim + 1 :])
    return jnp.moveaxis(parts, dim, 0)


def sum_at_owner(value, axis, dim):
    parts = split_up(value, dim, lax.axis_size(axis))
    arrived = lax.all_to_all(parts, axis, split_axis=0, concat_axis=0, tiled=True)
    return arrived.astype(jnp.float32).sum(axis=0)


def scaled_states(columns, energy, moment):
    factor = jnp.exp(-energy * moment)
    return (columns.astype(jnp.float32) * factor[:, None]).astype(jnp.bfloat16)


def slab_rows(orbitals, occ_scaled, emp_scaled, occ_count):
    dims = (((0,), (0,)), ((), ()))
    green_occ = lax.dot_general(
        orbitals[:occ_count], occ_scaled, dims, preferred_element_type=jnp.float32
    )
    green_emp = lax.dot_general(
        orbitals[occ_count:], emp_scaled, dims, preferred_element_type=jnp.float32
    )
    return green_occ * green_emp


def body(
    occ_rows,
    emp_rows,
    occ_cols,
    emp_cols,
    occ_energy,
    emp_energy,
    time_points,
    time_weights,
    frequencies,
    trial_vectors,
):
    occ_count = occ_rows.shape[0]
    time_index = lax.axis_index("tm")
    cos_table = time_weights[None, :] * jnp.cos(frequencies[:, None] * time_points[None, :])
    moment = lax.dynamic_index_in_dim(time_points, time_index, 0, keepdims=False)
    occ_scaled = scaled_states(occ_cols, occ_energy, moment)
    emp_scaled = scaled_states(emp_cols, emp_energy, moment)
    orbitals = jnp.concatenate([occ_rows, emp_rows], axis=0)
    gathered = gathered_by_axis(orbitals, COL, 1)
    polar = slab_rows(gathered, occ_scaled, emp_scaled, occ_count)
    reduced = sum_at_owner(
        jnp.dot(
            polar,
            trial_vectors,
            precision=lax.Precision.HIGHEST,
            preferred_element_type=jnp.float32,
        ).astype(jnp.bfloat16),
        COL,
        0,
    )
    column = lax.dynamic_index_in_dim(cos_table, time_index, 1, keepdims=False)
    return sum_at_owner((column[:, None, None] * reduced[None, :, :]).astype(jnp.bfloat16), "tm", 0)


def solution(mesh):
    torus = Mesh(mesh.devices.reshape(mesh.shape["tm"], 8, 2), ("tm", "col_0", "col_1"))
    in_specs = (
        P(None, COL),
        P(None, COL),
        P(None, COL),
        P(None, COL),
        P(),
        P(),
        P(),
        P(),
        P(),
        P(COL, None),
    )
    out_specs = P("tm", COL, None)
    return jax.shard_map(body, mesh=torus, in_specs=in_specs, out_specs=out_specs, check_vma=False)
```

profile of v0, /device:TPU:1, one launch (start us, length us, event | category | flops | bytes accessed | tf_op | source)
XLA Modules:
  0.0 155.8 jit_solution(10654744038027112074)
XLA Ops:
  6.5 0.0 copy-start
  6.5 0.0 all-gather.2.cloned.1.call-start
  6.5 1.1 pad_maximum_fusion
  7.7 7.5 %all_gather.6 = bf16[2048,128]{0,1:T(8,128)(2,1)} all-gather(bf16[2048,64]{0,1:T(8,128)(2,1)S(1)} %pad_maximum_fusion), channel_id=1, replica_groups=mesh['tm'=16,'col_0'=8,'col_1'=2] {'col_1'}, dimensions={1}, use_global_device_ids=true | all-gather | bytes 786432 | tf_op jit(solution)/shard_map/all_gather | solution.py:12
  15.2 0.0 all-gather.2.cloned.1.call-update
  15.2 1.2 dynamic-slice
  16.4 1.4 multiply_exponential_fusion
  17.8 57.3 %all-gather.2.cloned.1.call-done = bf16[2048,1024]{0,1:T(8,128)(2,1)} async-done(((bf16[2048,128]{0,1:T(8,128)(2,1)}), bf16[2048,1024]{0,1:T(8,128)(2,1)}) %all-gather.2.cloned.1.call-update) | async-done | bytes 4194320 | tf_op jit(solution)/shard_map/all_gather | solution.py:12
  75.1 0.0 copy-start.2
  75.1 0.0 copy-start.3
  75.1 4.8 %fusion.3 = f32[1024,1024]{1,0:T(8,128)S(1)} fusion(bf16[1024,1024]{1,0:T(8,128)(2,1)} %param.13, bf16[2048,1024]{0,1:T(8,128)(2,1)} %all-gather.2.cloned.1.call-done, f32[1024]{0:T(1024)S(1)} %get-tuple-element.5), kind=kOutput, calls=%fused_computation.5 | convolution fusion | flops 2150629376 | bytes 8392704 | tf_op jit(solution)/shard_map/dot_general | solution.py:38
  79.9 0.0 copy-done.2
  79.9 0.0 copy-done.3
  79.9 2.5 %fusion.2 = f32[1024,1024]{1,0:T(8,128)S(1)} fusion(bf16[1024,1024]{1,0:T(8,128)(2,1)S(1)} %copy-done.3, bf16[2048,1024]{0,1:T(8,128)(2,1)S(1)} %copy-done.2, f32[1024]{0:T(1024)S(1)} %get-tuple-element.6), kind=kOutput, calls=%fused_computation.4 | convolution fusion | flops 2150629376 | bytes 8392704 | tf_op jit(solution)/shard_map/dot_general | solution.py:35
  82.3 0.0 copy-done
  82.4 7.7 %fusion.8 = bf16[1024,512]{1,0:T(8,128)(2,1)} fusion(f32[1024,512]{1,0:T(8,128)S(1)} %copy-done, f32[1024,1024]{1,0:T(8,128)S(1)} %fusion.2, f32[1024,1024]{1,0:T(8,128)S(1)} %fusion.3), kind=kOutput, calls=%fused_computation.13 | convolution fusion | flops 6444023808 | bytes 11534336 | tf_op jit(solution)/shard_map/dot_general | solution.py:66
  90.0 0.0 copy-start.4
  90.0 0.0 copy-start.1
  90.0 5.2 %all-to-all-start = ((bf16[16,64,512]{2,1,0:T(8,128)(2,1)}), bf16[16,64,512]{2,1,0:T(8,128)(2,1)S(1)}, u32[]{:S(2)}, u32[]{:S(2)}) async-start(bf16[16,64,512]{2,1,0:T(8,128)(2,1)} %bitcast.6), calls=%async_computation | async-start | bytes 2097152 | tf_op jit(solution)/shard_map/all_to_all | solution.py:24
  95.2 0.0 copy-done.4
  95.2 0.7 dynamic-slice.1
  95.9 0.0 copy-done.1
  95.9 1.3 multiply_bitcast_fusion
  97.2 23.3 %all-to-all-done = bf16[16,64,512]{2,1,0:T(8,128)(2,1)S(1)} async-done(((bf16[16,64,512]{2,1,0:T(8,128)(2,1)}), bf16[16,64,512]{2,1,0:T(8,128)(2,1)S(1)}, u32[]{:S(2)}, u32[]{:S(2)}) %all-to-all-start) | async-done | bytes 1048608 | tf_op jit(solution)/shard_map/all_to_all | solution.py:24
  120.4 0.1 convert_reduce_fusion.1
  120.6 0.3 multiply_convert_fusion.4
  120.9 27.3 %all_to_all.10 = bf16[16,1,64,512]{3,2,1,0:T(8,128)(2,1)S(1)} all-to-all(bf16[16,1,64,512]{3,2,1,0:T(8,128)(2,1)S(1)} %multiply_convert_fusion.4), channel_id=1, replica_groups=mesh['tm'=16,'col_0'=8,'col_1'=2] {'tm'}, dimensions={0} | all-to-all | bytes 2097152 | tf_op jit(solution)/shard_map/all_to_all | solution.py:24
  148.2 0.8 convert_reduce_fusion
Async XLA Ops:
  6.5 75.8 %copy-start = (f32[1024,512]{1,0:T(8,128)S(1)}, f32[1024,512]{1,0:T(8,128)}, u32[]{:S(2)}) copy-start(f32[1024,512]{1,0:T(8,128)} %param.19) | copy-start | bytes 6291460
  6.5 68.5 %all-gather.2.cloned.1.call-start = ((), (), s32[]{:S(2)}) async-start(), calls=%async_computation.2 | async-start | bytes 4718592 | tf_op jit(solution)/shard_map/all_gather | solution.py:12
  75.1 4.8 %copy-start.2 = (bf16[2048,1024]{0,1:T(8,128)(2,1)S(1)}, bf16[2048,1024]{0,1:T(8,128)(2,1)}, u32[]{:S(2)}) copy-start(bf16[2048,1024]{0,1:T(8,128)(2,1)} %all-gather.2.cloned.1.call-done) | copy-start | bytes 12582916
  75.1 4.8 %copy-start.3 = (bf16[1024,1024]{1,0:T(8,128)(2,1)S(1)}, bf16[1024,1024]{1,0:T(8,128)(2,1)}, u32[]{:S(2)}) copy-start(bf16[1024,1024]{1,0:T(8,128)(2,1)} %param.12) | copy-start | bytes 6291460
  90.0 5.2 %copy-start.4 = (f32[16]{0:T(128)S(1)}, f32[16]{0:T(128)}, u32[]{:S(2)}) copy-start(f32[16]{0:T(128)} %param.17) | copy-start | bytes 196
  90.0 5.9 %copy-start.1 = (f32[16]{0:T(128)S(1)}, f32[16]{0:T(128)}, u32[]{:S(2)}) copy-start(f32[16]{0:T(128)} %param.18) | copy-start | bytes 196
  90.0 30.4 %all-to-all-start = ((bf16[16,64,512]{2,1,0:T(8,128)(2,1)}), bf16[16,64,512]{2,1,0:T(8,128)(2,1)S(1)}, u32[]{:S(2)}, u32[]{:S(2)}) async-start(bf16[16,64,512]{2,1,0:T(8,128)(2,1)} %bitcast.6), calls=%async_computation | async-start | bytes 2097152 | tf_op jit(solution)/shard_map/all_to_all | solution.py:24
Sparse Core Ops, SparseCore 0:
  15.3 59.7 all-gather.1
where the time goes:
time: 156 us
  waiting for transfers between devices  80.5 us (52%)
  blocking collectives  34.8 us (22%)
  matrix products  14.9 us (10%)
  between operations  13.5 us (9%)
  starting transfers between devices  5.18 us (3%)
  other arithmetic  5.01 us (3%)
  local copies, waits for them, and re-layouts  1.91 us (1%)
    all_gather x1, waiting for transfers between devices, gathered_by_axis(): value = lax.all_gather(value, axis, axis=dim, tiled=True)  57.3 us
    all_to_all x1, blocking collectives, sum_at_owner(): lax.all_to_all(parts, axis, split_axis=0, concat_axis=0, tiled=True)  27.3 us
    all_to_all x1, waiting for transfers between devices, sum_at_owner(): lax.all_to_all(parts, axis, split_axis=0, concat_axis=0, tiled=True)  23.3 us
    dot_general x1, matrix products, body(): jnp.dot(polar, trial_vectors, precision=lax.Precision.HIGHEST, preferred_...  7.67 us
    all_gather x1, blocking collectives, gathered_by_axis(): value = lax.all_gather(value, axis, axis=dim, tiled=True)  7.48 us
    all_to_all x1, starting transfers between devices, sum_at_owner(): lax.all_to_all(parts, axis, split_axis=0, concat_axis=0, tiled=True)  5.18 us
    dot_general x1, matrix products, slab_rows(): lax.dot_general(orbitals[occ_count:], emp_scaled, dims, preferred_element...  4.8 us
  transfers between devices with their start and end apart: 2, of which 2 were waited for; matrix products, arithmetic and copies ran while one was open for 3% of the time, Pallas kernels for 0%

commit v1 on v0

v1 whole, which is shorter than its diff:
```python
import jax
import jax.numpy as jnp
from jax import lax
from jax.sharding import Mesh
from jax.sharding import PartitionSpec as P


def body(
    occ_rows,
    emp_rows,
    occ_cols,
    emp_cols,
    occ_energy,
    emp_energy,
    time_points,
    time_weights,
    frequencies,
    trial_vectors,
):
    teams, peers = lax.axis_size("tm"), lax.axis_size("col")
    states, rows = occ_rows.shape
    trials = trial_vectors.shape[1]
    times = time_points.shape[0]
    share = rows // teams
    team = lax.axis_index("tm")

    both = jnp.stack([occ_rows.T, emp_rows.T]).reshape(2, teams, share, states)
    mine = lax.dynamic_index_in_dim(both, team, 1, keepdims=False)
    sent = jnp.broadcast_to(mine[None], (peers, 2, share, states)).reshape(peers, 2 * share, states)
    got = lax.all_to_all(sent, "col", split_axis=0, concat_axis=0, tiled=True)
    got = got.reshape(peers, 2, share, states)

    def green(rows_in, energy, columns):
        factor = jnp.exp(-energy[None, :] * time_points[:, None])
        scaled = rows_in.astype(jnp.float32)[:, None, :, :] * factor[None, :, None, :]
        scaled = scaled.astype(jnp.bfloat16).reshape(peers * times * share, states)
        return jnp.dot(scaled, columns, preferred_element_type=jnp.float32)

    polar = green(got[:, 0], occ_energy, occ_cols) * green(got[:, 1], emp_energy, emp_cols)
    partial = jnp.dot(
        polar, trial_vectors, precision=lax.Precision.HIGH, preferred_element_type=jnp.float32
    )
    partial = partial.astype(jnp.bfloat16).reshape(peers, times * share, trials)
    arrived = lax.all_to_all(partial, "col", split_axis=0, concat_axis=0, tiled=True)
    summed = arrived.astype(jnp.float32).sum(axis=0)

    cos_table = time_weights[None, :] * jnp.cos(frequencies[:, None] * time_points[None, :])
    freqs = frequencies.shape[0]
    spread = (cos_table[:, None, :, None] * jnp.eye(share)[None, :, None, :]).reshape(
        freqs * share, times * share
    )
    spectral = jnp.dot(
        spread, summed, precision=lax.Precision.HIGHEST, preferred_element_type=jnp.float32
    )
    out = lax.all_to_all(
        spectral.reshape(freqs, share, trials), "tm", split_axis=0, concat_axis=0, tiled=True
    )
    return out.reshape(1, rows, trials)


def solution(mesh):
    in_specs = (
        P(None, "col"),
        P(None, "col"),
        P(None, "col"),
        P(None, "col"),
        P(),
        P(),
        P(),
        P(),
        P(),
        P("col", None),
    )
    out_specs = P("tm", "col", None)
    return jax.shard_map(body, mesh=mesh, in_specs=in_specs, out_specs=out_specs, check_vma=False)
```

time: 156 us -> 96 us (0.62)
  waiting for transfers between devices: 80.5 us -> 32.5 us
  blocking collectives: 34.8 us -> 19.4 us
  between operations: 13.5 us -> 0.16 us
  local copies, waits for them, and re-layouts: 1.91 us -> 11.8 us
  starting transfers between devices: 5.18 us -> 13.8 us
  matrix products: 14.9 us -> 11.2 us
  other arithmetic: 5.01 us -> 6.61 us
    all_gather x1 -> x0, waiting for transfers between devices: 57.3 us -> none  [gathered_by_axis(): value = lax.all_gather(value, axis, axis=dim, tiled=True)]
    all_to_all x1 -> x2, waiting for transfers between devices: 23.3 us -> 32.5 us  [the longest x1 24 us: body(): lax.all_to_all(partial, 'col', split_axis=0, concat_axis=0, tiled=True)]
    all_to_all x1 -> x2, starting transfers between devices: 5.18 us -> 13.8 us  [the longest x1 10 us: body(): got = lax.all_to_all(sent, 'col', split_axis=0, concat_axis=0, tiled=True)]
    all_to_all x1, blocking collectives: 27.3 us -> 19.4 us  [body(): lax.all_to_all(spectral.reshape(freqs, share, trials), 'tm', split_axis=0...]
    convert_element_type x0 -> x2, local copies, waits for them, and re-layouts: none -> 7.89 us  [green(): scaled = scaled.astype(jnp.bfloat16).reshape(peers * times * share, states)]
    all_gather x1 -> x0, blocking collectives: 7.48 us -> none  [gathered_by_axis(): value = lax.all_gather(value, axis, axis=dim, tiled=True)]
    convert_element_type x1 -> x2, other arithmetic: 0.27 us -> 4.14 us  [the longest x1 4.14 us: green(): scaled = scaled.astype(jnp.bfloat16).reshape(peers * times * share, states)]
    dot_general x3 -> x4, matrix products: 14.9 us -> 11.2 us  [the longest x2 6.4 us: green(): return jnp.dot(scaled, columns, preferred_element_type=jnp.float32)]
where the time goes in v1:
time: 96 us; the launch traced here: 95.4 us
  waiting for transfers between devices  32.5 us (34%)
  blocking collectives  19.4 us (20%)
  starting transfers between devices  13.8 us (14%)
  local copies, waits for them, and re-layouts  11.8 us (12%)
  matrix products  11.2 us (12%)
  other arithmetic  6.61 us (7%)
    all_to_all x1, waiting for transfers between devices, body(): lax.all_to_all(partial, 'col', split_axis=0, concat_axis=0, tiled=True)  24 us
    all_to_all x1, blocking collectives, body(): lax.all_to_all(spectral.reshape(freqs, share, trials), 'tm', split_axis=0...  19.4 us
    all_to_all x1, starting transfers between devices, body(): got = lax.all_to_all(sent, 'col', split_axis=0, concat_axis=0, tiled=True)  10 us
    all_to_all x1, waiting for transfers between devices, body(): got = lax.all_to_all(sent, 'col', split_axis=0, concat_axis=0, tiled=True)  8.44 us
    convert_element_type x2, local copies, waits for them, and re-layouts, green(): scaled = scaled.astype(jnp.bfloat16).reshape(peers * times * share, states)  7.89 us
    dot_general x2, matrix products, green(): return jnp.dot(scaled, columns, preferred_element_type=jnp.float32)  6.4 us
    dot_general x1, matrix products, body(): jnp.dot(polar, trial_vectors, precision=lax.Precision.HIGH, preferred_ele...  4.49 us
    convert_element_type x1, other arithmetic, green(): scaled = scaled.astype(jnp.bfloat16).reshape(peers * times * share, states)  4.14 us
  transfers between devices with their start and end apart: 2, of which 2 were waited for; matrix products, arithmetic and copies ran while one was open for 3% of the time, Pallas kernels for 0%

profile of v1, /device:TPU:1, one launch (start us, length us, event | category | flops | bytes accessed | tf_op | source)
XLA Modules:
  0.0 95.4 jit_solution(4377084678956741466)
XLA Ops:
  0.0 0.0 copy-start
  0.0 1.1 %stack.10 = bf16[1,16,4,1024]{3,2,1,0:T(4,128)(2,1)S(1)} reshape(bf16[64,1024]{1,0:T(8,128)(2,1)} %bitcast.24) | data formatting | bytes 262144 | tf_op jit(solution)/shard_map/stack | solution.py:27
  1.1 1.0 %stack.9 = bf16[1,16,4,1024]{3,2,1,0:T(4,128)(2,1)S(1)} reshape(bf16[64,1024]{1,0:T(8,128)(2,1)} %bitcast.25) | data formatting | bytes 262144 | tf_op jit(solution)/shard_map/stack | solution.py:27
  2.1 0.7 broadcast_in_dim.5
  2.9 10.0 %all-to-all-start = ((bf16[16,8,1024]{2,1,0:T(8,128)(2,1)}), bf16[16,8,1024]{2,1,0:T(8,128)(2,1)S(1)}, u32[]{:S(2)}, u32[]{:S(2)}) async-start(bf16[16,8,1024]{2,1,0:T(8,128)(2,1)} %broadcast_in_dim.5), calls=%async_computation | async-start | bytes 524288 | tf_op jit(solution)/shard_map/all_to_all | solution.py:30
  12.9 0.7 neg.8
  13.6 0.7 neg.9
  14.3 0.7 multiply_exponential_fusion
  15.0 8.4 %all-to-all-done = bf16[16,8,1024]{2,1,0:T(8,128)(2,1)S(1)} async-done(((bf16[16,8,1024]{2,1,0:T(8,128)(2,1)}), bf16[16,8,1024]{2,1,0:T(8,128)(2,1)S(1)}, u32[]{:S(2)}, u32[]{:S(2)}) %all-to-all-start) | async-done | bytes 262176 | tf_op jit(solution)/shard_map/all_to_all | solution.py:30
  23.5 0.1 reshape.139
  23.6 0.1 fusion.5
  23.6 4.1 %multiply_convert_fusion = (bf16[16,16,4,1024]{3,2,1,0:T(4,128)(2,1)}, bf16[16,16,4,1024]{3,2,1,0:T(4,128)(2,1)}) fusion(f32[16,1024]{1,0:T(8,128)S(1)} %get-tuple-element.7, f32[16,4,1024]{2,1,0:T(4,128)S(1)} %get-tuple-element.5, f32[16,1024]{1,0:T(8,128)S(1)} %get-tuple-element.8, f32[16,4,1024]{2,1,0:T(4,128)S(1)} %get-tuple-element.6), kind=kLoop, calls=%fused_computation.2 | loop fusion | flops 4194304 | bytes 4849664 | tf_op jit(solution)/shard_map/convert_element_type | solution.py:36
  27.8 4.0 %convert_element_type.33 = bf16[1024,1024]{1,0:T(8,128)(2,1)} reshape(bf16[16,16,4,1024]{3,2,1,0:T(4,128)(2,1)} %get-tuple-element.10) | data formatting | bytes 4194304 | tf_op jit(solution)/shard_map/convert_element_type | solution.py:36
  31.7 3.9 %convert_element_type.35 = bf16[1024,1024]{1,0:T(8,128)(2,1)} reshape(bf16[16,16,4,1024]{3,2,1,0:T(4,128)(2,1)} %get-tuple-element.9) | data formatting | bytes 4194304 | tf_op jit(solution)/shard_map/convert_element_type | solution.py:36
  35.7 0.0 copy-done
  35.7 4.1 %fusion.14 = f32[1024,1024]{1,0:T(8,128)S(1)} fusion(bf16[1024,1024]{1,0:T(8,128)(2,1)} %convert_element_type.33, bf16[1024,1024]{1,0:T(8,128)(2,1)S(1)} %copy-done), kind=kOutput, calls=%fused_computation.23 | convolution fusion | flops 2147483648 | bytes 8388608 | tf_op jit(solution)/shard_map/dot_general | solution.py:37
  39.8 0.0 copy-done.1
  39.8 0.0 copy-done.6
  39.8 0.0 copy-start.2
  39.8 2.3 %fusion.15 = f32[1024,1024]{1,0:T(8,128)S(1)} fusion(bf16[1024,1024]{1,0:T(8,128)(2,1)S(1)} %copy-done.1, bf16[1024,1024]{1,0:T(8,128)(2,1)S(1)} %copy-done.6), kind=kOutput, calls=%fused_computation.24 | convolution fusion | flops 2147483648 | bytes 8388608 | tf_op jit(solution)/shard_map/dot_general | solution.py:37
  42.1 0.0 copy-done.2
  42.1 4.5 %fusion.2 = bf16[1024,512]{1,0:T(8,128)(2,1)} fusion(f32[1024,512]{1,0:T(8,128)S(1)} %copy-done.2, f32[1024,1024]{1,0:T(8,128)S(1)} %fusion.14, f32[1024,1024]{1,0:T(8,128)S(1)} %fusion.15), kind=kOutput, calls=%fused_computation.5 | convolution fusion | flops 3222798336 | bytes 11534336 | tf_op jit(solution)/shard_map/dot_general | solution.py:40
  46.6 3.8 %all-to-all-start.1 = ((bf16[16,64,512]{2,1,0:T(8,128)(2,1)}), bf16[16,64,512]{2,1,0:T(8,128)(2,1)S(1)}, u32[]{:S(2)}, u32[]{:S(2)}) async-start(bf16[16,64,512]{2,1,0:T(8,128)(2,1)} %bitcast.22), calls=%async_computation.1 | async-start | bytes 2097152 | tf_op jit(solution)/shard_map/all_to_all | solution.py:44
  50.5 0.1 cosine_multiply_fusion
  50.6 0.1 copy.13
  50.7 0.1 mul.136
  50.8 24.0 %all-to-all-done.1 = bf16[16,64,512]{2,1,0:T(8,128)(2,1)S(1)} async-done(((bf16[16,64,512]{2,1,0:T(8,128)(2,1)}), bf16[16,64,512]{2,1,0:T(8,128)(2,1)S(1)}, u32[]{:S(2)}, u32[]{:S(2)}) %all-to-all-start.1) | async-done | bytes 1048608 | tf_op jit(solution)/shard_map/all_to_all | solution.py:44
  74.8 0.1 convert_reduce_fusion
  75.0 0.3 fusion.7
  75.2 0.1 copy.14
  75.3 19.4 %all_to_all.15 = f32[16,4,512]{2,1,0:T(4,128)S(1)} all-to-all(f32[16,4,512]{2,1,0:T(4,128)S(1)} %copy.14), channel_id=1, replica_groups=mesh['tm'=16,'col'=16] {'tm'}, dimensions={0} | all-to-all | bytes 262144 | tf_op jit(solution)/shard_map/all_to_all | solution.py:55
  94.7 0.7 reshape.141
  (13 shorter events, 0.1 us)
Async XLA Ops:
  0.0 35.7 %copy-start = (bf16[1024,1024]{1,0:T(8,128)(2,1)S(1)}, bf16[1024,1024]{1,0:T(8,128)(2,1)}, u32[]{:S(2)}) copy-start(bf16[1024,1024]{1,0:T(8,128)(2,1)} %param.12) | copy-start | bytes 6291460
  2.9 20.6 %all-to-all-start = ((bf16[16,8,1024]{2,1,0:T(8,128)(2,1)}), bf16[16,8,1024]{2,1,0:T(8,128)(2,1)S(1)}, u32[]{:S(2)}, u32[]{:S(2)}) async-start(bf16[16,8,1024]{2,1,0:T(8,128)(2,1)} %broadcast_in_dim.5), calls=%async_computation | async-start | bytes 524288 | tf_op jit(solution)/shard_map/all_to_all | solution.py:30
  35.7 4.1 %copy-start.1 = (bf16[1024,1024]{1,0:T(8,128)(2,1)S(1)}, bf16[1024,1024]{1,0:T(8,128)(2,1)}, u32[]{:S(2)}) copy-start(bf16[1024,1024]{1,0:T(8,128)(2,1)} %convert_element_type.35) | copy-start | bytes 6291460
  35.7 4.1 %copy-start.6 = (bf16[1024,1024]{1,0:T(8,128)(2,1)S(1)}, bf16[1024,1024]{1,0:T(8,128)(2,1)}, u32[]{:S(2)}) copy-start(bf16[1024,1024]{1,0:T(8,128)(2,1)} %param.13) | copy-start | bytes 6291460
  39.8 2.4 %copy-start.2 = (f32[1024,512]{1,0:T(8,128)S(1)}, f32[1024,512]{1,0:T(8,128)}, u32[]{:S(2)}) copy-start(f32[1024,512]{1,0:T(8,128)} %param.19) | copy-start | bytes 6291460
  46.6 3.8 %copy-start.3 = (f32[16]{0:T(128)S(1)}, f32[16]{0:T(128)}, u32[]{:S(2)}) copy-start(f32[16]{0:T(128)} %param.16) | copy-start | bytes 196
  46.6 3.8 %copy-start.4 = (f32[16]{0:T(128)S(1)}, f32[16]{0:T(128)}, u32[]{:S(2)}) copy-start(f32[16]{0:T(128)} %param.18) | copy-start | bytes 196
  46.6 3.8 %copy-start.5 = (f32[16]{0:T(128)S(1)}, f32[16]{0:T(128)}, u32[]{:S(2)}) copy-start(f32[16]{0:T(128)} %param.17) | copy-start | bytes 196
  46.6 28.2 %all-to-all-start.1 = ((bf16[16,64,512]{2,1,0:T(8,128)(2,1)}), bf16[16,64,512]{2,1,0:T(8,128)(2,1)S(1)}, u32[]{:S(2)}, u32[]{:S(2)}) async-start(bf16[16,64,512]{2,1,0:T(8,128)(2,1)} %bitcast.22), calls=%async_computation.1 | async-start | bytes 2097152 | tf_op jit(solution)/shard_map/all_to_all | solution.py:44

commit v2 on v1

v2 whole, which is shorter than its diff:
```python
import functools

import jax
import jax.numpy as jnp
from jax import lax
from jax.experimental import pallas as pl
from jax.experimental.pallas import tpu as pltpu
from jax.sharding import Mesh
from jax.sharding import PartitionSpec as P

COL = ("z", "xl")
ALL = ("tm", "z", "xl")
F32, BF16 = jnp.float32, jnp.bfloat16
SMALL, LARGE = 12 << 20, 28 << 20


def pick_kernel(share, shares_ref, occ_ref, emp_ref, out_ref):
    rows = occ_ref.shape[0]
    line = lax.broadcasted_iota(jnp.int32, (2 * share, rows), 0)
    point = lax.broadcasted_iota(jnp.int32, (2 * share, rows), 1)
    for side in range(2):
        first = shares_ref[side] * share
        occ_pick = jnp.where((line < share) & (point == first + line), 1.0, 0.0).astype(BF16)
        emp_pick = jnp.where((line >= share) & (point == first + line - share), 1.0, 0.0)
        both = jnp.dot(occ_pick, occ_ref[...], preferred_element_type=F32)
        both += jnp.dot(emp_pick.astype(BF16), emp_ref[...], preferred_element_type=F32)
        both = both.astype(BF16)
        for peer in range(side, out_ref.shape[0], 2):
            out_ref[peer] = both


def pick(shares, occ_t, emp_t, peers, share):
    states = occ_t.shape[1]
    return pl.pallas_call(
        functools.partial(pick_kernel, share),
        out_shape=jax.ShapeDtypeStruct((peers, 2 * share, states), BF16),
        in_specs=[
            pl.BlockSpec(memory_space=pltpu.SMEM),
            pl.BlockSpec(memory_space=pltpu.VMEM),
            pl.BlockSpec(memory_space=pltpu.VMEM),
        ],
        out_specs=pl.BlockSpec(memory_space=pltpu.VMEM),
        compiler_params=pltpu.CompilerParams(vmem_limit_bytes=SMALL),
    )(shares, occ_t, emp_t)


def prepare_kernel(times_ref, energy_ref, trial_ref, factor_ref, high_ref, low_ref):
    for kind in range(2):
        factor_ref[kind] = jnp.exp(-energy_ref[kind : kind + 1, :] * times_ref[...])
    for start in range(0, trial_ref.shape[0], 256):
        value = trial_ref[start : start + 256, :]
        high = value.astype(BF16)
        high_ref[start : start + 256, :] = high
        low_ref[start : start + 256, :] = (value - high.astype(F32)).astype(BF16)


def prepare(times, energy, trial):
    states = energy.shape[1]
    return pl.pallas_call(
        prepare_kernel,
        out_shape=(
            jax.ShapeDtypeStruct((2, times.shape[0], states), F32),
            jax.ShapeDtypeStruct(trial.shape, BF16),
            jax.ShapeDtypeStruct(trial.shape, BF16),
        ),
        in_specs=[pl.BlockSpec(memory_space=pltpu.VMEM)] * 3,
        out_specs=(pl.BlockSpec(memory_space=pltpu.VMEM),) * 3,
        compiler_params=pltpu.CompilerParams(vmem_limit_bytes=SMALL),
    )(times, energy, trial)


def product_kernel(
    share, xl_ref, rows_ref, factor_ref, occ_ref, emp_ref, high_ref, low_ref, out_ref, occ_s, emp_s
):
    times = factor_ref.shape[1]
    block = pl.program_id(0)
    per_step = occ_s.shape[0] // (share * times)
    for index in range(per_step):
        peer = 2 * (block * per_step + index) + xl_ref[0]
        rows = rows_ref[peer].astype(F32)
        for r in range(share):
            at = (index * share + r) * times
            occ_s[at : at + times, :] = (rows[r : r + 1, :] * factor_ref[0]).astype(BF16)
            emp_s[at : at + times, :] = (
                rows[share + r : share + r + 1, :] * factor_ref[1]
            ).astype(BF16)
    polar = jnp.dot(occ_s[...], occ_ref[...], preferred_element_type=F32)
    polar *= jnp.dot(emp_s[...], emp_ref[...], preferred_element_type=F32)
    polar = polar.astype(BF16)
    total = jnp.dot(polar, high_ref[...], preferred_element_type=F32)
    total += jnp.dot(polar, low_ref[...], preferred_element_type=F32)
    out_ref[...] = total.astype(out_ref.dtype)


def products(xl, rows, factor, occ_cols, emp_cols, high, low, share, dtype):
    zs = rows.shape[0] // 2
    times, states = factor.shape[1:]
    trials = high.shape[1]
    per_step = 4
    lines = per_step * share * times
    whole = pl.BlockSpec(memory_space=pltpu.VMEM)
    columns = occ_cols.shape[1]
    flops = 2 * zs * share * times * columns * (2 * states + 2 * trials)
    return pl.pallas_call(
        functools.partial(product_kernel, share),
        grid=(zs // per_step,),
        out_shape=jax.ShapeDtypeStruct((zs * share * times, trials), dtype),
        in_specs=[pl.BlockSpec(memory_space=pltpu.SMEM)] + [whole] * 6,
        out_specs=pl.BlockSpec((lines, trials), lambda i: (i, 0)),
        scratch_shapes=[pltpu.VMEM((lines, states), BF16), pltpu.VMEM((lines, states), BF16)],
        compiler_params=pltpu.CompilerParams(vmem_limit_bytes=LARGE),
        cost_estimate=pl.CostEstimate(flops=flops, bytes_accessed=8 << 20, transcendentals=0),
    )(xl, rows, factor, occ_cols, emp_cols, high, low)


def x_pairs(zs):
    pairs = []
    for tm in range(16):
        for z in range(zs):
            for xl in range(2):
                other = tm ^ 2 if tm & 1 else tm
                pairs.append(((tm * zs + z) * 2 + xl, (other * zs + z) * 2 + 1 - xl))
    return pairs


def body(
    occ_rows,
    emp_rows,
    occ_cols,
    emp_cols,
    occ_energy,
    emp_energy,
    time_points,
    time_weights,
    frequencies,
    trial_vectors,
):
    teams, zs = lax.axis_size("tm"), lax.axis_size("z")
    peers = 2 * zs
    states, rows = occ_rows.shape
    trials = trial_vectors.shape[1]
    times = time_points.shape[0]
    freqs = frequencies.shape[0]
    share = rows // teams
    team, xl = lax.axis_index("tm"), lax.axis_index("xl")
    swapped = jnp.where(team & 1 == 1, team ^ 2, team)

    sent = pick(jnp.stack([team, swapped]), occ_rows.T, emp_rows.T, peers, share)
    got = lax.all_to_all(sent, COL, split_axis=0, concat_axis=0, tiled=True)

    energy = jnp.stack([occ_energy, emp_energy])
    factor, high, low = prepare(time_points[:, None], energy, trial_vectors)
    other = products(
        (1 - xl)[None], got, factor, occ_cols, emp_cols, high, low, share, BF16
    )
    arrived = lax.ppermute(other, ALL, x_pairs(zs))
    own = products(xl[None], got, factor, occ_cols, emp_cols, high, low, share, F32)
    pair = (own + arrived.astype(F32)).astype(BF16).reshape(zs, share * times, trials)
    summed = lax.all_to_all(pair, "z", split_axis=0, concat_axis=0, tiled=True)
    summed = summed.astype(F32).sum(axis=0)

    cos_table = time_weights[None, :] * jnp.cos(frequencies[:, None] * time_points[None, :])
    spread = (jnp.eye(share)[None, :, :, None] * cos_table[:, None, None, :]).reshape(
        freqs * share, share * times
    )
    spectral = jnp.dot(spread, summed, precision=lax.Precision.HIGHEST, preferred_element_type=F32)
    out = lax.all_to_all(
        spectral.reshape(freqs, share, trials), "tm", split_axis=0, concat_axis=0, tiled=True
    )
    by_share = out.reshape(teams // 4, 2, 2, share, trials)
    turned = jnp.stack([by_share[:, :, 0], by_share[:, ::-1, 1]], axis=2)
    out = jnp.where(xl == 1, turned, by_share)
    return out.reshape(1, rows, trials)


def solution(mesh):
    torus = Mesh(mesh.devices.reshape(mesh.shape["tm"], mesh.shape["col"] // 2, 2), ALL)
    in_specs = (
        P(None, COL),
        P(None, COL),
        P(None, COL),
        P(None, COL),
        P(),
        P(),
        P(),
        P(),
        P(),
        P(COL, None),
    )
    out_specs = P("tm", COL, None)
    return jax.shard_map(body, mesh=torus, in_specs=in_specs, out_specs=out_specs, check_vma=False)
```

time: 96 us -> 78.4 us (0.82)
  blocking collectives: 19.4 us -> 0 us
  matrix products: 11.2 us -> 0.27 us
  starting transfers between devices: 13.8 us -> 23.9 us
  Pallas kernels: 0 us -> 9.21 us
  other arithmetic: 6.61 us -> 2.68 us
  local copies, waits for them, and re-layouts: 11.8 us -> 9.05 us
    all_to_all x1 -> x0, blocking collectives: 19.4 us -> none  [body(): lax.all_to_all(spectral.reshape(freqs, share, trials), 'tm', split_axis=0...]
    dot_general x3 -> x0, matrix products: 10.9 us -> none  [the longest x2 6.4 us: green(): return jnp.dot(scaled, columns, preferred_element_type=jnp.float32)]
    pallas_call x0 -> x4, Pallas kernels: none -> 9.21 us  [the longest x2 7.22 us: products(): pl.pallas_call(functools.partial(product_kernel, share), grid=(zs // per_...]
    all_to_all x2 -> x3, starting transfers between devices: 13.8 us -> 22.3 us  [the longest x1 10 us: body(): got = lax.all_to_all(sent, COL, split_axis=0, concat_axis=0, tiled=True)]
    convert_element_type x2 -> x0, local copies, waits for them, and re-layouts: 7.89 us -> none  [green(): scaled = scaled.astype(jnp.bfloat16).reshape(peers * times * share, states)]
    unnamed x14 -> x22, local copies, waits for them, and re-layouts: 0.03 us -> 7.21 us
    ppermute x0 -> x1, waiting for transfers between devices: none -> 4.12 us  [body(): arrived = lax.ppermute(other, ALL, x_pairs(zs))]
    all_to_all x2 -> x3, waiting for transfers between devices: 32.5 us -> 28.5 us  [the longest x1 14.9 us: body(): summed = lax.all_to_all(pair, 'z', split_axis=0, concat_axis=0, tiled=True)]
  transfers between devices with their start and end apart: 2 -> 4, of which waited for: 2 -> 4; matrix products, arithmetic and copies ran while one was open for 3% -> 2% of each run, Pallas kernels for 0% -> 5%
where the time goes in v2:
time: 78.4 us; the launch traced here: 77.9 us
  waiting for transfers between devices  32.6 us (42%)
  starting transfers between devices  23.9 us (30%)
  Pallas kernels  9.21 us (12%)
  local copies, waits for them, and re-layouts  9.05 us (12%)
  other arithmetic  2.68 us (3%)
    all_to_all x1, waiting for transfers between devices, body(): summed = lax.all_to_all(pair, 'z', split_axis=0, concat_axis=0, tiled=True)  14.9 us
    all_to_all x1, starting transfers between devices, body(): got = lax.all_to_all(sent, COL, split_axis=0, concat_axis=0, tiled=True)  10 us
    all_to_all x1, starting transfers between devices, body(): lax.all_to_all(spectral.reshape(freqs, share, trials), 'tm', split_axis=0...  8.77 us
    all_to_all x1, waiting for transfers between devices, body(): lax.all_to_all(spectral.reshape(freqs, share, trials), 'tm', split_axis=0...  7.62 us
    pallas_call x2, Pallas kernels, products(): pl.pallas_call(functools.partial(product_kernel, share), grid=(zs // per_...  7.22 us
    unnamed x22, local copies, waits for them, and re-layouts  7.21 us
    all_to_all x1, waiting for transfers between devices, body(): got = lax.all_to_all(sent, COL, split_axis=0, concat_axis=0, tiled=True)  6 us
    ppermute x1, waiting for transfers between devices, body(): arrived = lax.ppermute(other, ALL, x_pairs(zs))  4.12 us
  transfers between devices with their start and end apart: 4, of which 4 were waited for; matrix products, arithmetic and copies ran while one was open for 2% of the time, Pallas kernels for 5%

profile of v2, /device:TPU:1, one launch (start us, length us, event | category | flops | bytes accessed | tf_op | source)
XLA Modules:
  0.0 77.9 jit_solution(1009616524289232006)
XLA Ops:
  0.0 0.1 pad_add_fusion.shares_ref
  0.1 0.9 %copy-done.1 = bf16[1024,64]{0,1:T(8,128)(2,1)S(1)} copy-done((bf16[1024,64]{0,1:T(8,128)(2,1)S(1)}, bf16[1024,64]{0,1:T(8,128)(2,1)}, u32[]{:S(2)}) %copy-start.1) | copy-done | bytes 131096
  1.0 0.9 %copy-done.2 = bf16[1024,64]{0,1:T(8,128)(2,1)S(1)} copy-done((bf16[1024,64]{0,1:T(8,128)(2,1)S(1)}, bf16[1024,64]{0,1:T(8,128)(2,1)}, u32[]{:S(2)}) %copy-start.2) | copy-done | bytes 131096
  1.9 1.5 %shard_map.100 = bf16[16,8,1024]{2,1,0:T(8,128)(2,1)} custom-call(s32[2]{0:T(128)S(1)} %pad_add_fusion.shares_ref, bf16[64,1024]{1,0:T(8,128)(2,1)S(1)} %bitcast.14, bf16[64,1024]{1,0:T(8,128)(2,1)S(1)} %bitcast.15), custom_call_target="tpu_custom_call" | custom-call | tf_op jit(solution)/shard_map/pallas_call | solution.py:34
  3.3 10.0 %all-to-all-start = ((bf16[16,8,1024]{2,1,0:T(8,128)(2,1)}), bf16[16,8,1024]{2,1,0:T(8,128)(2,1)S(1)}, u32[]{:S(2)}, u32[]{:S(2)}) async-start(bf16[16,8,1024]{2,1,0:T(8,128)(2,1)} %shard_map.100), calls=%async_computation | async-start | bytes 524288 | tf_op jit(solution)/shard_map/all_to_all | solution.py:149
  13.4 0.7 copy.16.times_ref
  14.1 0.7 pad_maximum_fusion.1.energy_ref
  14.8 0.0 copy-start
  14.8 1.6 %copy-done = f32[1024,512]{1,0:T(8,128)S(1)} copy-done((f32[1024,512]{1,0:T(8,128)S(1)}, f32[1024,512]{1,0:T(8,128)}, u32[]{:S(2)}) %copy-start) | copy-done | bytes 2097176
  16.4 0.5 shard_map.101
  17.0 1.0 %copy-done.6 = bf16[1024,512]{1,0:T(8,128)(2,1)} copy-done((bf16[1024,512]{1,0:T(8,128)(2,1)}, bf16[1024,512]{1,0:T(8,128)(2,1)S(1)}, u32[]{:S(2)}) %copy-start.6) | copy-done | bytes 1048600
  18.0 6.0 %all-to-all-done.rows_ref = bf16[16,8,1024]{2,1,0:T(8,128)(2,1)S(1)} async-done(((bf16[16,8,1024]{2,1,0:T(8,128)(2,1)}), bf16[16,8,1024]{2,1,0:T(8,128)(2,1)S(1)}, u32[]{:S(2)}, u32[]{:S(2)}) %all-to-all-start) | async-done | bytes 262176 | tf_op jit(solution)/shard_map/all_to_all | solution.py:149
  24.0 1.6 %copy-done.4 = bf16[1024,1024]{1,0:T(8,128)(2,1)S(1)} copy-done((bf16[1024,1024]{1,0:T(8,128)(2,1)S(1)}, bf16[1024,1024]{1,0:T(8,128)(2,1)}, u32[]{:S(2)}) %copy-start.4) | copy-done | bytes 2097176
  25.6 1.2 %copy-done.7 = bf16[1024,512]{1,0:T(8,128)(2,1)S(1)} copy-done((bf16[1024,512]{1,0:T(8,128)(2,1)S(1)}, bf16[1024,512]{1,0:T(8,128)(2,1)}, u32[]{:S(2)}) %copy-start.7) | copy-done | bytes 1048600
  26.8 3.6 %shard_map.103 = bf16[512,512]{1,0:T(8,128)(2,1)S(1)} custom-call(s32[1]{0:T(128)} %bitcast.8.xl_ref, bf16[16,8,1024]{2,1,0:T(8,128)(2,1)S(1)} %all-to-all-done.rows_ref, f32[2,16,1024]{2,1,0:T(8,128)S(1)} %get-tuple-element.8.factor_ref, bf16[1024,1024]{1,0:T(8,128)(2,1)S(1)} %copy-done.3, bf16[1024,1024]{1,0:T(8,128)(2,1)S(1)} %copy-done.4, ...), custom_call_target="tpu_custom_call" | custom-call | flops 3221225472 | bytes 8388608 | tf_op jit(solution)/shard_map/pallas_call | solution.py:104
  30.4 1.6 %collective-permute-start = (bf16[512,512]{1,0:T(8,128)(2,1)S(1)}, bf16[512,512]{1,0:T(8,128)(2,1)S(1)}, u32[]{:S(2)}, u32[]{:S(2)}) collective-permute-start(bf16[512,512]{1,0:T(8,128)(2,1)S(1)} %shard_map.103), channel_id=1, source_target_pairs={{0,1},{1,0},{2,3},{3,2},{4,5},{5,4},{6,7},{7,6},{8,9},{9,8},{10,11... | collective-permute-start | bytes 1572872 | tf_op jit(solution)/shard_map/ppermute | solution.py:156
  32.0 3.6 %shard_map.102 = f32[512,512]{1,0:T(8,128)S(1)} custom-call(s32[1]{0:T(128)} %bitcast.xl_ref, bf16[16,8,1024]{2,1,0:T(8,128)(2,1)S(1)} %all-to-all-done.rows_ref, f32[2,16,1024]{2,1,0:T(8,128)S(1)} %get-tuple-element.8.factor_ref, bf16[1024,1024]{1,0:T(8,128)(2,1)S(1)} %copy-done.3, bf16[1024,1024]{1,0:T(8,128)(2,1)S(1)} %copy-done.5, ...), custom_call_target="tpu_custom_call" | custom-call | flops 3221225472 | bytes 8388608 | tf_op jit(solution)/shard_map/pallas_call | solution.py:104
  35.6 0.0 copy-start.8
  35.6 4.1 %collective-permute-done = bf16[512,512]{1,0:T(8,128)(2,1)S(1)} collective-permute-done((bf16[512,512]{1,0:T(8,128)(2,1)S(1)}, bf16[512,512]{1,0:T(8,128)(2,1)S(1)}, u32[]{:S(2)}, u32[]{:S(2)}) %collective-permute-start) | collective-permute-done | bytes 524320 | tf_op jit(solution)/shard_map/ppermute | solution.py:156
  39.7 1.0 %add_convert_fusion = bf16[512,512]{1,0:T(8,128)(2,1)} fusion(f32[512,512]{1,0:T(8,128)S(1)} %shard_map.102, bf16[512,512]{1,0:T(8,128)(2,1)S(1)} %collective-permute-done), kind=kLoop, calls=%fused_computation.1 | loop fusion | flops 786432 | bytes 2097152 | tf_op jit(solution)/shard_map/convert_element_type | solution.py:158
  40.7 3.5 %all-to-all-start.1 = ((bf16[8,64,512]{2,1,0:T(8,128)(2,1)}), bf16[8,64,512]{2,1,0:T(8,128)(2,1)S(1)}, u32[]{:S(2)}, u32[]{:S(2)}) async-start(bf16[8,64,512]{2,1,0:T(8,128)(2,1)} %bitcast.9), calls=%async_computation.1 | async-start | bytes 1048576 | tf_op jit(solution)/shard_map/all_to_all | solution.py:159
  44.2 0.1 cosine_multiply_fusion
  44.4 0.1 mul.61
  44.5 0.1 mul.52
  44.5 0.1 mul.53
  44.6 14.9 %all-to-all-done.1 = bf16[8,64,512]{2,1,0:T(8,128)(2,1)S(1)} async-done(((bf16[8,64,512]{2,1,0:T(8,128)(2,1)}), bf16[8,64,512]{2,1,0:T(8,128)(2,1)S(1)}, u32[]{:S(2)}, u32[]{:S(2)}) %all-to-all-start.1) | async-done | bytes 524320 | tf_op jit(solution)/shard_map/all_to_all | solution.py:159
  59.5 0.1 convert_reduce_fusion
  59.6 0.3 fusion
  59.9 0.7 copy.17
  60.6 8.8 %all-to-all-start.2 = ((f32[16,4,512]{2,1,0:T(4,128)}), f32[16,4,512]{2,1,0:T(4,128)S(1)}, u32[]{:S(2)}, u32[]{:S(2)}) async-start(f32[16,4,512]{2,1,0:T(4,128)} %copy.17), calls=%async_computation.2 | async-start | bytes 262144 | tf_op jit(solution)/shard_map/all_to_all | solution.py:167
  69.4 7.6 %all-to-all-done.2 = f32[16,4,512]{2,1,0:T(4,128)S(1)} async-done(((f32[16,4,512]{2,1,0:T(4,128)}), f32[16,4,512]{2,1,0:T(4,128)S(1)}, u32[]{:S(2)}, u32[]{:S(2)}) %all-to-all-start.2) | async-done | bytes 131104 | tf_op jit(solution)/shard_map/all_to_all | solution.py:167
  77.2 0.7 broadcast_select_fusion
  (21 shorter events, 0.2 us)
Async XLA Ops:
  0.1 0.9 %copy-start.1 = (bf16[1024,64]{0,1:T(8,128)(2,1)S(1)}, bf16[1024,64]{0,1:T(8,128)(2,1)}, u32[]{:S(2)}) copy-start(bf16[1024,64]{0,1:T(8,128)(2,1)} %param.10) | copy-start | bytes 393220
  1.0 0.9 %copy-start.2 = (bf16[1024,64]{0,1:T(8,128)(2,1)S(1)}, bf16[1024,64]{0,1:T(8,128)(2,1)}, u32[]{:S(2)}) copy-start(bf16[1024,64]{0,1:T(8,128)(2,1)} %param.11) | copy-start | bytes 393220
  3.3 20.6 %all-to-all-start = ((bf16[16,8,1024]{2,1,0:T(8,128)(2,1)}), bf16[16,8,1024]{2,1,0:T(8,128)(2,1)S(1)}, u32[]{:S(2)}, u32[]{:S(2)}) async-start(bf16[16,8,1024]{2,1,0:T(8,128)(2,1)} %shard_map.100), calls=%async_computation | async-start | bytes 524288 | tf_op jit(solution)/shard_map/all_to_all | solution.py:149
  14.8 1.6 %copy-start = (f32[1024,512]{1,0:T(8,128)S(1)}, f32[1024,512]{1,0:T(8,128)}, u32[]{:S(2)}) copy-start(f32[1024,512]{1,0:T(8,128)} %trial_ref.1) | copy-start | bytes 6291460
  16.4 7.5 %copy-start.3 = (bf16[1024,1024]{1,0:T(8,128)(2,1)S(1)}, bf16[1024,1024]{1,0:T(8,128)(2,1)}, u32[]{:S(2)}) copy-start(bf16[1024,1024]{1,0:T(8,128)(2,1)} %occ_ref.3) | copy-start | bytes 6291460
  17.0 1.0 %copy-start.6 = (bf16[1024,512]{1,0:T(8,128)(2,1)}, bf16[1024,512]{1,0:T(8,128)(2,1)S(1)}, u32[]{:S(2)}) copy-start(bf16[1024,512]{1,0:T(8,128)(2,1)S(1)} %get-tuple-element.10.low_ref) | copy-start | bytes 3145732
  24.0 1.6 %copy-start.4 = (bf16[1024,1024]{1,0:T(8,128)(2,1)S(1)}, bf16[1024,1024]{1,0:T(8,128)(2,1)}, u32[]{:S(2)}) copy-start(bf16[1024,1024]{1,0:T(8,128)(2,1)} %emp_ref.3) | copy-start | bytes 6291460
  25.5 1.2 %copy-start.7 = (bf16[1024,512]{1,0:T(8,128)(2,1)S(1)}, bf16[1024,512]{1,0:T(8,128)(2,1)}, u32[]{:S(2)}) copy-start(bf16[1024,512]{1,0:T(8,128)(2,1)} %copy-done.6) | copy-start | bytes 3145732
  26.8 5.2 %copy-start.5 = (bf16[1024,1024]{1,0:T(8,128)(2,1)S(1)}, bf16[1024,1024]{1,0:T(8,128)(2,1)}, u32[]{:S(2)}) copy-start(bf16[1024,1024]{1,0:T(8,128)(2,1)} %emp_ref.3) | copy-start | bytes 6291460
  30.4 9.3 %collective-permute-start = (bf16[512,512]{1,0:T(8,128)(2,1)S(1)}, bf16[512,512]{1,0:T(8,128)(2,1)S(1)}, u32[]{:S(2)}, u32[]{:S(2)}) collective-permute-start(bf16[512,512]{1,0:T(8,128)(2,1)S(1)} %shard_map.103), channel_id=1, source_target_pairs={{0,1},{1,0},{2,3},{3,2},{4,5},{5,4},{6,7},{7,6},{8,9},{9,8},{10,11... | collective-permute-start | bytes 1572872 | tf_op jit(solution)/shard_map/ppermute | solution.py:156
  35.6 8.6 %copy-start.8 = (f32[16]{0:T(128)S(1)}, f32[16]{0:T(128)}, u32[]{:S(2)}) copy-start(f32[16]{0:T(128)} %param.16) | copy-start | bytes 196
  35.6 8.6 %copy-start.9 = (f32[16]{0:T(128)S(1)}, f32[16]{0:T(128)}, u32[]{:S(2)}) copy-start(f32[16]{0:T(128)} %param.18) | copy-start | bytes 196
  35.6 8.6 %copy-start.10 = (f32[16]{0:T(128)S(1)}, f32[16]{0:T(128)}, u32[]{:S(2)}) copy-start(f32[16]{0:T(128)} %param.17) | copy-start | bytes 196
  40.7 18.8 %all-to-all-start.1 = ((bf16[8,64,512]{2,1,0:T(8,128)(2,1)}), bf16[8,64,512]{2,1,0:T(8,128)(2,1)S(1)}, u32[]{:S(2)}, u32[]{:S(2)}) async-start(bf16[8,64,512]{2,1,0:T(8,128)(2,1)} %bitcast.9), calls=%async_computation.1 | async-start | bytes 1048576 | tf_op jit(solution)/shard_map/all_to_all | solution.py:159
  60.6 16.4 %all-to-all-start.2 = ((f32[16,4,512]{2,1,0:T(4,128)}), f32[16,4,512]{2,1,0:T(4,128)S(1)}, u32[]{:S(2)}, u32[]{:S(2)}) async-start(f32[16,4,512]{2,1,0:T(4,128)} %copy.17), calls=%async_computation.2 | async-start | bytes 262144 | tf_op jit(solution)/shard_map/all_to_all | solution.py:167

commit v3 on v2

v3 whole, which is shorter than its diff:
```python
import functools

import jax
import jax.numpy as jnp
from jax import lax
from jax.experimental import pallas as pl
from jax.experimental.pallas import tpu as pltpu
from jax.sharding import Mesh
from jax.sharding import PartitionSpec as P

COL = ("z", "xl")
ALL = ("tm", "z", "xl")
F32, BF16 = jnp.float32, jnp.bfloat16
SMALL, LARGE = 12 << 20, 20 << 20
BLOCK = 4


def far_ref(value):
    return pltpu.with_memory_space_constraint(value, pltpu.HBM)


def pick_kernel(share, shares_ref, occ_ref, emp_ref, out_ref, held, sems):
    copies = []
    for side in range(2):
        near = pl.multiple_of(shares_ref[side] * share // 8 * 8, 8)
        for kind, ref in enumerate((occ_ref, emp_ref)):
            copies.append(
                pltpu.make_async_copy(
                    ref.at[pl.ds(near, 8)], held.at[2 * side + kind], sems.at[2 * side + kind]
                )
            )
    for copy in copies:
        copy.start()
    line = lax.broadcasted_iota(jnp.int32, (2 * share, 8), 0)
    point = lax.broadcasted_iota(jnp.int32, (2 * share, 8), 1)
    for side in range(2):
        first = lax.rem(shares_ref[side] * share, 8)
        occ_pick = jnp.where((line < share) & (point == first + line), 1.0, 0.0).astype(BF16)
        emp_pick = jnp.where((line >= share) & (point == first + line - share), 1.0, 0.0)
        copies[2 * side].wait()
        copies[2 * side + 1].wait()
        both = jnp.dot(occ_pick, held[2 * side], preferred_element_type=F32)
        both += jnp.dot(emp_pick.astype(BF16), held[2 * side + 1], preferred_element_type=F32)
        both = both.astype(BF16)
        for peer in range(side, out_ref.shape[0], 2):
            out_ref[peer] = both


def pick(shares, occ_t, emp_t, peers, share):
    states = occ_t.shape[1]
    return pl.pallas_call(
        functools.partial(pick_kernel, share),
        out_shape=jax.ShapeDtypeStruct((peers, 2 * share, states), BF16),
        in_specs=[
            pl.BlockSpec(memory_space=pltpu.SMEM),
            pl.BlockSpec(memory_space=pltpu.HBM),
            pl.BlockSpec(memory_space=pltpu.HBM),
        ],
        out_specs=pl.BlockSpec(memory_space=pltpu.VMEM),
        scratch_shapes=[pltpu.VMEM((4, 8, states), BF16), pltpu.SemaphoreType.DMA((4,))],
        compiler_params=pltpu.CompilerParams(vmem_limit_bytes=SMALL),
    )(shares, far_ref(occ_t), far_ref(emp_t))


def halves(value):
    high = value.astype(BF16)
    return high, (value - high.astype(F32)).astype(BF16)


def prepare_kernel(
    times_ref,
    weights_ref,
    freqs_ref,
    occ_energy_ref,
    emp_energy_ref,
    trial_ref,
    factor_ref,
    high_ref,
    low_hbm,
    spread_ref,
    low_ref,
    sem,
):
    for start in range(0, trial_ref.shape[0], 256):
        at = slice(start, start + 256)
        high_ref[at, :], low_ref[at, :] = halves(trial_ref[at, :])
    copy = pltpu.make_async_copy(low_ref, low_hbm, sem)
    copy.start()
    times, freqs = times_ref.shape[0], freqs_ref.shape[0]
    for kind, ref in enumerate((occ_energy_ref, emp_energy_ref)):
        for t in range(times):
            factor_ref[kind, t : t + 1, :] = jnp.exp(-ref[...] * times_ref[t])
    lines = spread_ref.shape[1]
    points = lines // times
    line = lax.broadcasted_iota(jnp.int32, (freqs, lines), 0)
    lane = lax.broadcasted_iota(jnp.int32, (freqs, lines), 1)
    moment, weight, freq = (jnp.zeros((freqs, lines), F32) for _ in range(3))
    for t in range(times):
        moment = jnp.where(lane % times == t, times_ref[t], moment)
        weight = jnp.where(lane % times == t, weights_ref[t], weight)
    for k in range(freqs):
        freq = jnp.where(line == k, freqs_ref[k], freq)
    table = weight * jnp.cos(freq * moment)
    point = lax.broadcasted_iota(jnp.int32, (points, lines), 0)
    same = lax.broadcasted_iota(jnp.int32, (points, lines), 1) // times == point
    for k in range(freqs):
        main, rest = halves(jnp.where(same, table[k : k + 1, :], 0.0))
        spread_ref[0, k * points : (k + 1) * points, :] = main
        spread_ref[1, k * points : (k + 1) * points, :] = rest
    copy.wait()


def prepare(times, weights, freqs, occ_energy, emp_energy, trial, points):
    states = occ_energy.shape[0]
    few = pl.BlockSpec(memory_space=pltpu.SMEM)
    whole = pl.BlockSpec(memory_space=pltpu.VMEM)
    return pl.pallas_call(
        prepare_kernel,
        out_shape=(
            jax.ShapeDtypeStruct((2, times.shape[0], states), F32),
            jax.ShapeDtypeStruct(trial.shape, BF16),
            jax.ShapeDtypeStruct(trial.shape, BF16),
            jax.ShapeDtypeStruct((2, freqs.shape[0] * points, points * times.shape[0]), BF16),
        ),
        in_specs=[few, few, few, whole, whole, whole],
        out_specs=(whole, whole, pl.BlockSpec(memory_space=pltpu.HBM), whole),
        scratch_shapes=[pltpu.VMEM(trial.shape, BF16), pltpu.SemaphoreType.DMA],
        compiler_params=pltpu.CompilerParams(vmem_limit_bytes=SMALL),
    )(*map(far_ref, (times, weights, freqs, occ_energy[None, :], emp_energy[None, :], trial)))


def product_kernel(
    share,
    first,
    xl_ref,
    rows_ref,
    factor_ref,
    occ_ref,
    emp_hbm,
    high_ref,
    low_hbm,
    out_ref,
    occ_s,
    emp_s,
    emp_ref,
    low_ref,
    sems,
):
    times = factor_ref.shape[1]
    step = pl.program_id(0)
    emp_copy = pltpu.make_async_copy(emp_hbm, emp_ref, sems.at[0])
    low_copy = pltpu.make_async_copy(low_hbm, low_ref, sems.at[1])

    @pl.when(step == 0)
    def _():
        emp_copy.start()
        low_copy.start()

    for index in range(BLOCK):
        peer = 2 * (first + step * BLOCK + index) + xl_ref[0]
        rows = rows_ref[peer].astype(F32)
        for r in range(share):
            at = (index * share + r) * times
            occ_s[at : at + times, :] = (rows[r : r + 1, :] * factor_ref[0]).astype(BF16)
            emp_s[at : at + times, :] = (
                rows[share + r : share + r + 1, :] * factor_ref[1]
            ).astype(BF16)
    polar = jnp.dot(occ_s[...], occ_ref[...], preferred_element_type=F32)

    @pl.when(step == 0)
    def _():
        emp_copy.wait()

    polar *= jnp.dot(emp_s[...], emp_ref[...], preferred_element_type=F32)
    polar = polar.astype(BF16)

    @pl.when(step == 0)
    def _():
        low_copy.wait()

    total = jnp.dot(polar, high_ref[...], preferred_element_type=F32)
    total += jnp.dot(polar, low_ref[...], preferred_element_type=F32)
    out_ref[...] = total.astype(out_ref.dtype)


def products(xl, rows, factor, occ_cols, emp_cols, high, low, share, first, count, dtype):
    times, states = factor.shape[1:]
    columns, trials = high.shape
    lines = BLOCK * share * times
    whole = pl.BlockSpec(memory_space=pltpu.VMEM)
    far = pl.BlockSpec(memory_space=pltpu.HBM)
    flops = 2 * count * share * times * columns * (2 * states + 2 * trials)
    return pl.pallas_call(
        functools.partial(product_kernel, share, first),
        grid=(count // BLOCK,),
        out_shape=jax.ShapeDtypeStruct((count * share * times, trials), dtype),
        in_specs=[
            pl.BlockSpec(memory_space=pltpu.SMEM),
            whole,
            whole,
            whole,
            far,
            whole,
            far,
        ],
        out_specs=pl.BlockSpec((lines, trials), lambda i: (i, 0)),
        scratch_shapes=[
            pltpu.VMEM((lines, states), BF16),
            pltpu.VMEM((lines, states), BF16),
            pltpu.VMEM(emp_cols.shape, BF16),
            pltpu.VMEM(low.shape, BF16),
            pltpu.SemaphoreType.DMA((2,)),
        ],
        compiler_params=pltpu.CompilerParams(vmem_limit_bytes=LARGE),
        cost_estimate=pl.CostEstimate(flops=flops, bytes_accessed=8 << 20, transcendentals=0),
    )(xl, rows, factor, occ_cols, far_ref(emp_cols), high, far_ref(low))


def mix_kernel(share, own_ref, low_half_ref, high_half_ref, spread_ref, out_ref):
    spread, spread_rest = spread_ref[0], spread_ref[1]
    lines = spread_ref.shape[1]
    freqs = lines // (BLOCK * share)
    zs = out_ref.shape[0] // freqs
    for step, part_ref in enumerate((low_half_ref, high_half_ref)):
        total = own_ref[step * lines : (step + 1) * lines, :] + part_ref[...].astype(F32)
        main, rest = halves(total)
        mixed = jnp.dot(spread, rest, preferred_element_type=F32)
        mixed += jnp.dot(spread_rest, main, preferred_element_type=F32)
        mixed += jnp.dot(spread, main, preferred_element_type=F32)
        mixed = mixed.astype(BF16)
        for k in range(freqs):
            for index in range(BLOCK):
                at = (k * BLOCK + index) * share
                out_ref[k * zs + step * BLOCK + index] = mixed[at : at + share, :]


def mix(own, low_half, high_half, spread, share):
    lines, trials = own.shape
    return pl.pallas_call(
        functools.partial(mix_kernel, share),
        out_shape=jax.ShapeDtypeStruct((lines // share, share, trials), BF16),
        in_specs=[pl.BlockSpec(memory_space=pltpu.VMEM)] * 4,
        out_specs=pl.BlockSpec(memory_space=pltpu.VMEM),
        compiler_params=pltpu.CompilerParams(vmem_limit_bytes=SMALL),
    )(own, low_half, high_half, spread)


def collect_kernel(turn_ref, got_ref, out_ref):
    teams, share = out_ref.shape[:2]
    zs = got_ref.shape[0] // teams
    for place in range(teams):
        source = place ^ turn_ref[0] if place & 1 else place
        total = got_ref[source * zs].astype(F32)
        for z in range(1, zs):
            total += got_ref[source * zs + z].astype(F32)
        out_ref[place] = total


def collect(turn, got, teams):
    share, trials = got.shape[1:]
    return pl.pallas_call(
        collect_kernel,
        out_shape=jax.ShapeDtypeStruct((teams, share, trials), F32),
        in_specs=[
            pl.BlockSpec(memory_space=pltpu.SMEM),
            pl.BlockSpec(memory_space=pltpu.VMEM),
        ],
        out_specs=pl.BlockSpec(memory_space=pltpu.VMEM),
        compiler_params=pltpu.CompilerParams(vmem_limit_bytes=SMALL),
    )(turn, got)


def x_pairs(zs):
    pairs = []
    for tm in range(16):
        for z in range(zs):
            for xl in range(2):
                other = tm ^ 2 if tm & 1 else tm
                pairs.append(((tm * zs + z) * 2 + xl, (other * zs + z) * 2 + 1 - xl))
    return pairs


def body(
    occ_rows,
    emp_rows,
    occ_cols,
    emp_cols,
    occ_energy,
    emp_energy,
    time_points,
    time_weights,
    frequencies,
    trial_vectors,
):
    teams, zs = lax.axis_size("tm"), lax.axis_size("z")
    peers = 2 * zs
    states, rows = occ_rows.shape
    trials = trial_vectors.shape[1]
    share = rows // teams
    team, xl = lax.axis_index("tm"), lax.axis_index("xl")
    swapped = jnp.where(team & 1 == 1, team ^ 2, team)

    sent = pick(jnp.stack([team, swapped]), occ_rows.T, emp_rows.T, peers, share)
    got = lax.all_to_all(sent, COL, split_axis=0, concat_axis=0, tiled=True)

    factor, high, low, spread = prepare(
        time_points, time_weights, frequencies, occ_energy, emp_energy, trial_vectors, BLOCK * share
    )

    def part(side, first, count, dtype):
        return products(
            side[None], got, factor, occ_cols, emp_cols, high, low, share, first, count, dtype
        )

    pairs = x_pairs(zs)
    low_half = lax.ppermute(part(1 - xl, 0, BLOCK, BF16), ALL, pairs)
    high_half = lax.ppermute(part(1 - xl, BLOCK, BLOCK, BF16), ALL, pairs)
    own = part(xl, 0, zs, F32)
    sent = mix(own, low_half, high_half, spread, share)
    got = lax.all_to_all(sent, ("tm", "z"), split_axis=0, concat_axis=0, tiled=True)
    out = collect((2 * xl)[None], got, teams)
    return out.reshape(1, rows, trials)


def solution(mesh):
    torus = Mesh(mesh.devices.reshape(mesh.shape["tm"], mesh.shape["col"] // 2, 2), ALL)
    in_specs = (
        P(None, COL),
        P(None, COL),
        P(None, COL),
        P(None, COL),
        P(),
        P(),
        P(),
        P(),
        P(),
        P(COL, None),
    )
    out_specs = P("tm", COL, None)
    return jax.shard_map(body, mesh=torus, in_specs=in_specs, out_specs=out_specs, check_vma=False)
```

time: 78.4 us -> 71.1 us (0.907)
  Pallas kernels: 9.21 us -> 18.3 us
  local copies, waits for them, and re-layouts: 9.05 us -> 2.39 us
  waiting for transfers between devices: 32.6 us -> 26.6 us
  other arithmetic: 2.68 us -> 0.07 us
    pallas_call x2 -> x5, Pallas kernels: 7.22 us -> 13.7 us  [the longest x3 12.3 us: products(): pl.pallas_call(functools.partial(product_kernel, share, first), grid=(cou...]
    unnamed x22 -> x8, local copies, waits for them, and re-layouts: 7.21 us -> 1.68 us
    ppermute x1 -> x2, waiting for transfers between devices: 4.12 us -> 0.01 us  [the longest x1 0.01 us: body(): low_half = lax.ppermute(part(1 - xl, 0, BLOCK, BF16), ALL, pairs)]
    all_to_all x2 -> x1, waiting for transfers between devices: 22.5 us -> 19.9 us  [body(): lax.all_to_all(sent, ('tm', 'z'), split_axis=0, concat_axis=0, tiled=True)]
    all_to_all x2 -> x1, starting transfers between devices: 12.3 us -> 10.4 us  [body(): lax.all_to_all(sent, ('tm', 'z'), split_axis=0, concat_axis=0, tiled=True)]
    pallas_call x1, Pallas kernels: 0.53 us -> 2.26 us  [prepare(): pl.pallas_call(prepare_kernel, out_shape=(jax.ShapeDtypeStruct((2, times....]
    ppermute x1 -> x2, starting transfers between devices: 1.56 us -> 2.85 us  [the longest x1 1.56 us: body(): high_half = lax.ppermute(part(1 - xl, BLOCK, BLOCK, BF16), ALL, pairs)]
    convert_element_type x2 -> x0, other arithmetic: 0.99 us -> none  [the longest x1 0.99 us: body(): (own + arrived.astype(F32)).astype(BF16).reshape(zs, share * times, trials)]
  transfers between devices with their start and end apart: 4 -> 4, of which waited for: 4 -> 2; matrix products, arithmetic and copies ran while one was open for 2% -> 0% of each run, Pallas kernels for 5% -> 16%
where the time goes in v3:
time: 71.1 us; the launch traced here: 70.8 us
  waiting for transfers between devices  26.6 us (37%)
  starting transfers between devices  23.3 us (33%)
  Pallas kernels  18.3 us (26%)
  local copies, waits for them, and re-layouts  2.39 us (3%)
    all_to_all x1, waiting for transfers between devices, body(): lax.all_to_all(sent, ('tm', 'z'), split_axis=0, concat_axis=0, tiled=True)  19.9 us
    pallas_call x3, Pallas kernels, products(): pl.pallas_call(functools.partial(product_kernel, share, first), grid=(cou...  12.3 us
    all_to_all x1, starting transfers between devices, body(): lax.all_to_all(sent, ('tm', 'z'), split_axis=0, concat_axis=0, tiled=True)  10.4 us
    all_to_all x1, starting transfers between devices, body(): got = lax.all_to_all(sent, COL, split_axis=0, concat_axis=0, tiled=True)  10 us
    all_to_all x1, waiting for transfers between devices, body(): got = lax.all_to_all(sent, COL, split_axis=0, concat_axis=0, tiled=True)  6.61 us
    pallas_call x1, Pallas kernels, pick(): pl.pallas_call(functools.partial(pick_kernel, share), out_shape=jax.Shape...  2.35 us
    pallas_call x1, Pallas kernels, prepare(): pl.pallas_call(prepare_kernel, out_shape=(jax.ShapeDtypeStruct((2, times....  2.26 us
    unnamed x8, local copies, waits for them, and re-layouts  1.68 us
  transfers between devices with their start and end apart: 4, of which 2 were waited for; matrix products, arithmetic and copies ran while one was open for 0% of the time, Pallas kernels for 16%

profile of v3, /device:TPU:1, one launch (start us, length us, event | category | flops | bytes accessed | tf_op | source)
XLA Modules:
  0.0 70.8 jit_solution(12494519003412823081)
XLA Ops:
  0.0 0.0 copy-start
  0.0 0.1 pad_add_fusion.shares_ref
  0.1 2.3 %shard_map.100 = bf16[16,8,1024]{2,1,0:T(8,128)(2,1)} custom-call(s32[2]{0:T(128)S(1)} %pad_add_fusion.shares_ref, bf16[64,1024]{1,0:T(8,128)(2,1)} %bitcast.9, bf16[64,1024]{1,0:T(8,128)(2,1)} %bitcast.10), custom_call_target="tpu_custom_call" | custom-call | tf_op jit(solution)/shard_map/pallas_call | solution.py:51
  2.4 10.0 %all-to-all-start = ((bf16[16,8,1024]{2,1,0:T(8,128)(2,1)}), bf16[16,8,1024]{2,1,0:T(8,128)(2,1)S(1)}, u32[]{:S(2)}, u32[]{:S(2)}) async-start(bf16[16,8,1024]{2,1,0:T(8,128)(2,1)} %shard_map.100), calls=%async_computation | async-start | bytes 524288 | tf_op jit(solution)/shard_map/all_to_all | solution.py:304
  12.5 2.3 %shard_map.101 = (f32[2,16,1024]{2,1,0:T(8,128)S(1)}, bf16[1024,512]{1,0:T(8,128)(2,1)S(1)}, bf16[1024,512]{1,0:T(8,128)(2,1)S(1)}, bf16[2,256,256]{2,1,0:T(8,128)(2,1)S(1)}) custom-call(f32[16]{0:T(128)} %times_ref.1, f32[16]{0:T(128)} %weights_ref.1, f32[16]{0:T(128)} %freqs_ref.1, f32[1,1024]{1,0:T(1,128)} %bitcast.11, f32[1,1024]{1,0:T(1,128)} %bitcast.12, ...), custom_call_target="tpu_custom_call" | custom-call | tf_op jit(solution)/shard_map/pallas_call | solution.py:117
  14.8 0.0 copy-start.1
  14.8 1.0 %copy-done.1 = bf16[1024,512]{1,0:T(8,128)(2,1)} copy-done((bf16[1024,512]{1,0:T(8,128)(2,1)}, bf16[1024,512]{1,0:T(8,128)(2,1)S(1)}, u32[]{:S(2)}) %copy-start.1) | copy-done | bytes 1048600
  15.7 0.0 copy-start.2
  15.7 0.7 %copy-done.2 = bf16[2,256,256]{2,1,0:T(8,128)(2,1)} copy-done((bf16[2,256,256]{2,1,0:T(8,128)(2,1)}, bf16[2,256,256]{2,1,0:T(8,128)(2,1)S(1)}, u32[]{:S(2)}) %copy-start.2) | copy-done | bytes 262168
  16.4 6.6 %all-to-all-done.rows_ref = bf16[16,8,1024]{2,1,0:T(8,128)(2,1)S(1)} async-done(((bf16[16,8,1024]{2,1,0:T(8,128)(2,1)}), bf16[16,8,1024]{2,1,0:T(8,128)(2,1)S(1)}, u32[]{:S(2)}, u32[]{:S(2)}) %all-to-all-start) | async-done | bytes 262176 | tf_op jit(solution)/shard_map/all_to_all | solution.py:304
  23.1 0.0 copy-done
  23.1 3.5 %shard_map.104 = bf16[256,512]{1,0:T(8,128)(2,1)S(1)} custom-call(s32[1]{0:T(128)} %bitcast.8.xl_ref, bf16[16,8,1024]{2,1,0:T(8,128)(2,1)S(1)} %all-to-all-done.rows_ref, f32[2,16,1024]{2,1,0:T(8,128)S(1)} %get-tuple-element.9.factor_ref, bf16[1024,1024]{1,0:T(8,128)(2,1)S(1)} %copy-done, bf16[1024,1024]{1,0:T(8,128)(2,1)} %emp_hbm.5, ...), custom_call_target="tpu_custom_call" | custom-call | flops 1610612736 | bytes 8388608 | tf_op jit(solution)/shard_map/pallas_call | solution.py:193
  26.6 1.6 %collective-permute-start.1 = (bf16[256,512]{1,0:T(8,128)(2,1)S(1)}, bf16[256,512]{1,0:T(8,128)(2,1)S(1)}, u32[]{:S(2)}, u32[]{:S(2)}) collective-permute-start(bf16[256,512]{1,0:T(8,128)(2,1)S(1)} %shard_map.104), channel_id=1, source_target_pairs={{0,1},{1,0},{2,3},{3,2},{4,5},{5,4},{6,7},{7,6},{8,9},{9,8},{10,11... | collective-permute-start | bytes 786440 | tf_op jit(solution)/shard_map/ppermute | solution.py:317
  28.1 3.5 %shard_map.103 = bf16[256,512]{1,0:T(8,128)(2,1)S(1)} custom-call(s32[1]{0:T(128)} %bitcast.8.xl_ref, bf16[16,8,1024]{2,1,0:T(8,128)(2,1)S(1)} %all-to-all-done.rows_ref, f32[2,16,1024]{2,1,0:T(8,128)S(1)} %get-tuple-element.9.factor_ref, bf16[1024,1024]{1,0:T(8,128)(2,1)S(1)} %copy-done, bf16[1024,1024]{1,0:T(8,128)(2,1)} %emp_hbm.5, ...), custom_call_target="tpu_custom_call" | custom-call | flops 1610612736 | bytes 8388608 | tf_op jit(solution)/shard_map/pallas_call | solution.py:193
  31.7 1.3 %collective-permute-start = (bf16[256,512]{1,0:T(8,128)(2,1)S(1)}, bf16[256,512]{1,0:T(8,128)(2,1)S(1)}, u32[]{:S(2)}, u32[]{:S(2)}) collective-permute-start(bf16[256,512]{1,0:T(8,128)(2,1)S(1)} %shard_map.103), channel_id=1, source_target_pairs={{0,1},{1,0},{2,3},{3,2},{4,5},{5,4},{6,7},{7,6},{8,9},{9,8},{10,11... | collective-permute-start | bytes 786440 | tf_op jit(solution)/shard_map/ppermute | solution.py:316
  33.0 0.0 copy-start.3
  33.0 5.2 %shard_map.102.own_ref = f32[512,512]{1,0:T(8,128)S(1)} custom-call(s32[1]{0:T(128)} %bitcast.1.xl_ref, bf16[16,8,1024]{2,1,0:T(8,128)(2,1)S(1)} %all-to-all-done.rows_ref, f32[2,16,1024]{2,1,0:T(8,128)S(1)} %get-tuple-element.9.factor_ref, bf16[1024,1024]{1,0:T(8,128)(2,1)S(1)} %copy-done, bf16[1024,1024]{1,0:T(8,128)(2,1)} %emp_hbm.5, ...), custom_call_target="tpu_custom_call" | custom-call | flops 3221225472 | bytes 8388608 | tf_op jit(solution)/shard_map/pallas_call | solution.py:193
  38.2 0.0 collective-permute-done.1.high_half_ref
  38.2 0.0 collective-permute-done.low_half_ref
  38.2 0.0 copy-done.3
  38.2 1.4 %shard_map.105 = bf16[128,4,512]{2,1,0:T(4,128)(2,1)} custom-call(f32[512,512]{1,0:T(8,128)S(1)} %shard_map.102.own_ref, bf16[256,512]{1,0:T(8,128)(2,1)S(1)} %collective-permute-done.low_half_ref, bf16[256,512]{1,0:T(8,128)(2,1)S(1)} %collective-permute-done.1.high_half_ref, bf16[2,256,256]{2,1,0:T(8,128)(2,1)S(1)} %copy-done.3), custom_call_target="tpu_custom_call" | custom-call | tf_op jit(solution)/shard_map/pallas_call | solution.py:239
  39.6 10.4 %all-to-all-start.1 = ((bf16[128,4,512]{2,1,0:T(4,128)(2,1)}), bf16[128,4,512]{2,1,0:T(4,128)(2,1)S(1)}, u32[]{:S(2)}, u32[]{:S(2)}) async-start(bf16[128,4,512]{2,1,0:T(4,128)(2,1)} %shard_map.105), calls=%async_computation.1 | async-start | bytes 1048576 | tf_op jit(solution)/shard_map/all_to_all | solution.py:320
  50.0 19.9 %all-to-all-done.1.got_ref = bf16[128,4,512]{2,1,0:T(4,128)(2,1)S(1)} async-done(((bf16[128,4,512]{2,1,0:T(4,128)(2,1)}), bf16[128,4,512]{2,1,0:T(4,128)(2,1)S(1)}, u32[]{:S(2)}, u32[]{:S(2)}) %all-to-all-start.1) | async-done | bytes 524320 | tf_op jit(solution)/shard_map/all_to_all | solution.py:320
  70.0 0.1 shard_map.106
  70.1 0.7 reshape.3
Async XLA Ops:
  0.0 23.1 %copy-start = (bf16[1024,1024]{1,0:T(8,128)(2,1)S(1)}, bf16[1024,1024]{1,0:T(8,128)(2,1)}, u32[]{:S(2)}) copy-start(bf16[1024,1024]{1,0:T(8,128)(2,1)} %occ_ref.5) | copy-start | bytes 6291460
  2.4 20.6 %all-to-all-start = ((bf16[16,8,1024]{2,1,0:T(8,128)(2,1)}), bf16[16,8,1024]{2,1,0:T(8,128)(2,1)S(1)}, u32[]{:S(2)}, u32[]{:S(2)}) async-start(bf16[16,8,1024]{2,1,0:T(8,128)(2,1)} %shard_map.100), calls=%async_computation | async-start | bytes 524288 | tf_op jit(solution)/shard_map/all_to_all | solution.py:304
  14.8 1.0 %copy-start.1 = (bf16[1024,512]{1,0:T(8,128)(2,1)}, bf16[1024,512]{1,0:T(8,128)(2,1)S(1)}, u32[]{:S(2)}) copy-start(bf16[1024,512]{1,0:T(8,128)(2,1)S(1)} %get-tuple-element.11.low_hbm) | copy-start | bytes 3145732
  15.7 0.7 %copy-start.2 = (bf16[2,256,256]{2,1,0:T(8,128)(2,1)}, bf16[2,256,256]{2,1,0:T(8,128)(2,1)S(1)}, u32[]{:S(2)}) copy-start(bf16[2,256,256]{2,1,0:T(8,128)(2,1)S(1)} %get-tuple-element.12.spread_ref) | copy-start | bytes 786436
  26.6 11.6 %collective-permute-start.1 = (bf16[256,512]{1,0:T(8,128)(2,1)S(1)}, bf16[256,512]{1,0:T(8,128)(2,1)S(1)}, u32[]{:S(2)}, u32[]{:S(2)}) collective-permute-start(bf16[256,512]{1,0:T(8,128)(2,1)S(1)} %shard_map.104), channel_id=1, source_target_pairs={{0,1},{1,0},{2,3},{3,2},{4,5},{5,4},{6,7},{7,6},{8,9},{9,8},{10,11... | collective-permute-start | bytes 786440 | tf_op jit(solution)/shard_map/ppermute | solution.py:317
  31.7 6.5 %collective-permute-start = (bf16[256,512]{1,0:T(8,128)(2,1)S(1)}, bf16[256,512]{1,0:T(8,128)(2,1)S(1)}, u32[]{:S(2)}, u32[]{:S(2)}) collective-permute-start(bf16[256,512]{1,0:T(8,128)(2,1)S(1)} %shard_map.103), channel_id=1, source_target_pairs={{0,1},{1,0},{2,3},{3,2},{4,5},{5,4},{6,7},{7,6},{8,9},{9,8},{10,11... | collective-permute-start | bytes 786440 | tf_op jit(solution)/shard_map/ppermute | solution.py:316
  33.0 5.2 %copy-start.3 = (bf16[2,256,256]{2,1,0:T(8,128)(2,1)S(1)}, bf16[2,256,256]{2,1,0:T(8,128)(2,1)}, u32[]{:S(2)}) copy-start(bf16[2,256,256]{2,1,0:T(8,128)(2,1)} %copy-done.2) | copy-start | bytes 786436
  39.6 30.3 %all-to-all-start.1 = ((bf16[128,4,512]{2,1,0:T(4,128)(2,1)}), bf16[128,4,512]{2,1,0:T(4,128)(2,1)S(1)}, u32[]{:S(2)}, u32[]{:S(2)}) async-start(bf16[128,4,512]{2,1,0:T(4,128)(2,1)} %shard_map.105), calls=%async_computation.1 | async-start | bytes 1048576 | tf_op jit(solution)/shard_map/all_to_all | solution.py:320

commit v4 on v0

v4 whole, which is shorter than its diff:
```python
import functools

import jax
import jax.numpy as jnp
from jax import lax
from jax.experimental import pallas as pl
from jax.experimental.pallas import tpu as pltpu
from jax.sharding import Mesh
from jax.sharding import PartitionSpec as P

COL = ("zh", "zl", "xl")
ALL = ("tm",) + COL
F32, BF16 = jnp.float32, jnp.bfloat16
FEW = pl.BlockSpec(memory_space=pltpu.SMEM)
WHOLE = pl.BlockSpec(memory_space=pltpu.VMEM)
SMALL, LARGE = 12 << 20, 20 << 20
BLOCK = 4
PICKCOST = 1 << 35


def far_ref(value):
    return pltpu.with_memory_space_constraint(value, pltpu.HBM)


def pick_kernel(
    share,
    times_hbm,
    occ_energy_hbm,
    emp_energy_hbm,
    occ_hbm,
    emp_hbm,
    out_ref,
    factor_ref,
    held,
    times_ref,
    energy_ref,
    sems,
):
    team = lax.axis_index("tm")
    shares = team, jnp.where(team & 1 == 1, team ^ 2, team)
    pairs = []
    for side in range(2):
        near = pl.multiple_of(shares[side] * share // 8 * 8, 8)
        for kind, ref in enumerate((occ_hbm, emp_hbm)):
            pairs.append((ref.at[pl.ds(near, 8)], held.at[2 * side + kind]))
    pairs.append((times_hbm, times_ref))
    pairs.append((occ_energy_hbm, energy_ref.at[0]))
    pairs.append((emp_energy_hbm, energy_ref.at[1]))
    copies = [pltpu.make_async_copy(*pair, sems.at[i]) for i, pair in enumerate(pairs)]
    for copy in copies:
        copy.start()
    line = lax.broadcasted_iota(jnp.int32, (2 * share, 8), 0)
    point = lax.broadcasted_iota(jnp.int32, (2 * share, 8), 1)
    for side in range(2):
        first = lax.rem(shares[side] * share, 8)
        occ_pick = jnp.where((line < share) & (point == first + line), 1.0, 0.0).astype(BF16)
        emp_pick = jnp.where((line >= share) & (point == first + line - share), 1.0, 0.0)
        copies[2 * side].wait()
        copies[2 * side + 1].wait()
        both = jnp.dot(occ_pick, held[2 * side], preferred_element_type=F32)
        both += jnp.dot(emp_pick.astype(BF16), held[2 * side + 1], preferred_element_type=F32)
        both = both.astype(BF16)
        for peer in range(side, out_ref.shape[0], 2):
            out_ref[peer] = both
    for copy in copies[4:7]:
        copy.wait()
    times = times_ref.shape[1]
    row = lax.broadcasted_iota(jnp.int32, (times, times), 0)
    lane = lax.broadcasted_iota(jnp.int32, (times, times), 1)
    moments = jnp.sum(jnp.where(row == lane, times_ref[...], 0.0), axis=1, keepdims=True)
    for kind in range(2):
        factor_ref[kind] = jnp.exp(-energy_ref[kind] * moments)


def pick(times, occ_energy, emp_energy, occ_t, emp_t, peers, share):
    states = occ_t.shape[1]
    far = pl.BlockSpec(memory_space=pltpu.HBM)
    count = times.shape[0]
    return pl.pallas_call(
        functools.partial(pick_kernel, share),
        out_shape=(
            jax.ShapeDtypeStruct((peers, 2 * share, states), BF16),
            jax.ShapeDtypeStruct((2, count, states), F32),
        ),
        in_specs=[far] * 5,
        out_specs=(WHOLE,) * 2,
        scratch_shapes=[
            pltpu.VMEM((4, 8, states), BF16),
            pltpu.VMEM((1, count), F32),
            pltpu.VMEM((2, 1, states), F32),
            pltpu.SemaphoreType.DMA((7,)),
        ],
        compiler_params=pltpu.CompilerParams(vmem_limit_bytes=SMALL),
        cost_estimate=pl.CostEstimate(flops=PICKCOST, bytes_accessed=1 << 20, transcendentals=0),
    )(
        far_ref(times[None, :]),
        far_ref(occ_energy[None, :]),
        far_ref(emp_energy[None, :]),
        far_ref(occ_t),
        far_ref(emp_t),
    )


def halves(value):
    high = value.astype(BF16)
    return high, (value - high.astype(F32)).astype(BF16)


def scale(share, part, rows_ref, factor_ref, scaled):
    times = factor_ref.shape[1]
    occ_s, emp_s = scaled
    start = 2 * (lax.axis_index("zl") ^ (part >> 1)) + (lax.axis_index("xl") ^ (part & 1))
    for index in range(BLOCK):
        rows = rows_ref[4 * index + start].astype(F32)
        for r in range(share):
            at = (index * share + r) * times
            occ_s[at : at + times, :] = (rows[r : r + 1, :] * factor_ref[0]).astype(BF16)
            emp_s[at : at + times, :] = (
                rows[share + r : share + r + 1, :] * factor_ref[1]
            ).astype(BF16)


def first_kernel(
    share,
    part,
    rows_ref,
    factor_ref,
    occ_ref,
    emp_ref,
    trial_ref,
    out_ref,
    high_ref,
    low_ref,
    *scaled,
):
    for begin in range(0, trial_ref.shape[0], 256):
        at = slice(begin, begin + 256)
        high_ref[at, :], low_ref[at, :] = halves(trial_ref[at, :])
    next_kernel(
        share, part, rows_ref, factor_ref, occ_ref, emp_ref, high_ref, low_ref, out_ref, *scaled
    )


def next_kernel(
    share, part, rows_ref, factor_ref, occ_ref, emp_ref, high_ref, low_ref, out_ref, *scaled
):
    scale(share, part, rows_ref, factor_ref, scaled)
    polar = jnp.dot(scaled[0][...], occ_ref[...], preferred_element_type=F32)
    polar *= jnp.dot(scaled[1][...], emp_ref[...], preferred_element_type=F32)
    polar = polar.astype(BF16)
    total = jnp.dot(polar, high_ref[...], preferred_element_type=F32)
    total += jnp.dot(polar, low_ref[...], preferred_element_type=F32)
    out_ref[...] = total.astype(out_ref.dtype)


def table_kernel(share, part, times_ref, weights_ref, freqs_ref, *refs):
    times, freqs = times_ref.shape[0], freqs_ref.shape[0]
    points = BLOCK * share
    lines = points * times
    line = lax.broadcasted_iota(jnp.int32, (freqs, lines), 0)
    lane = lax.broadcasted_iota(jnp.int32, (freqs, lines), 1)
    moment, weight, freq = (jnp.zeros((freqs, lines), F32) for _ in range(3))
    for t in range(times):
        moment = jnp.where(lane % times == t, times_ref[t], moment)
        weight = jnp.where(lane % times == t, weights_ref[t], weight)
    for k in range(freqs):
        freq = jnp.where(line == k, freqs_ref[k], freq)
    table = weight * jnp.cos(freq * moment)
    point = lax.broadcasted_iota(jnp.int32, (points, lines), 0)
    same = lax.broadcasted_iota(jnp.int32, (points, lines), 1) // times == point
    *inputs, out_ref, spread_ref, occ_s, emp_s = refs
    for k in range(freqs):
        main, rest = halves(jnp.where(same, table[k : k + 1, :], 0.0))
        spread_ref[0, k * points : (k + 1) * points, :] = main
        spread_ref[1, k * points : (k + 1) * points, :] = rest
    next_kernel(share, part, *inputs, out_ref, occ_s, emp_s)


def cost(lines, states, columns, trials):
    return pl.CostEstimate(
        flops=4 * lines * columns * (states + trials), bytes_accessed=8 << 20, transcendentals=0
    )


def first_products(part, rows, factor, occ_cols, emp_cols, trial, share):
    states, columns = occ_cols.shape
    lines, trials = BLOCK * share * factor.shape[1], trial.shape[1]
    return pl.pallas_call(
        functools.partial(first_kernel, share, part),
        out_shape=(
            jax.ShapeDtypeStruct((lines, trials), BF16),
            jax.ShapeDtypeStruct(trial.shape, BF16),
            jax.ShapeDtypeStruct(trial.shape, BF16),
        ),
        in_specs=[WHOLE] * 5,
        out_specs=(WHOLE,) * 3,
        scratch_shapes=[pltpu.VMEM((lines, states), BF16)] * 2,
        compiler_params=pltpu.CompilerParams(vmem_limit_bytes=LARGE),
        cost_estimate=cost(lines, states, columns, trials),
    )(rows, factor, occ_cols, emp_cols, trial)


def next_products(part, rows, factor, occ_cols, emp_cols, high, low, share, dtype, grid=None):
    times, states = factor.shape[1:]
    columns, trials = high.shape
    lines = BLOCK * share * times
    out = jax.ShapeDtypeStruct((lines, trials), dtype)
    grid = () if grid is None else grid
    return pl.pallas_call(
        functools.partial(table_kernel if grid else next_kernel, share, part),
        out_shape=(out, jax.ShapeDtypeStruct((2, lines, lines), BF16)) if grid else out,
        in_specs=[FEW] * len(grid) + [WHOLE] * 6,
        out_specs=(WHOLE, WHOLE) if grid else WHOLE,
        scratch_shapes=[pltpu.VMEM((lines, states), BF16)] * 2,
        compiler_params=pltpu.CompilerParams(vmem_limit_bytes=LARGE),
        cost_estimate=cost(lines, states, columns, trials),
    )(*grid, rows, factor, occ_cols, emp_cols, high, low)


def mix_kernel(share, spread_ref, own_ref, x_ref, z_ref, out_ref):
    total = own_ref[...] + x_ref[...].astype(F32) + z_ref[...].astype(F32)
    main, rest = halves(total)
    mixed = jnp.dot(spread_ref[0], rest, preferred_element_type=F32)
    mixed += jnp.dot(spread_ref[1], main, preferred_element_type=F32)
    mixed += jnp.dot(spread_ref[0], main, preferred_element_type=F32)
    mixed = mixed.astype(BF16)
    for place in range(out_ref.shape[0]):
        out_ref[place] = mixed[place * share : (place + 1) * share, :]


def mix(spread, own, from_x, from_z, share):
    lines, trials = own.shape
    return pl.pallas_call(
        functools.partial(mix_kernel, share),
        out_shape=jax.ShapeDtypeStruct((lines // share, share, trials), BF16),
        in_specs=[WHOLE] * 4,
        out_specs=WHOLE,
        compiler_params=pltpu.CompilerParams(vmem_limit_bytes=SMALL),
    )(spread, own, from_x, from_z)


def collect_kernel(teams, got_ref, out_ref):
    share = got_ref.shape[1]
    zs = got_ref.shape[0] // teams
    turn = 2 * lax.axis_index("xl")
    for place in range(teams):
        source = place ^ turn if place & 1 else place
        total = got_ref[source * zs].astype(F32)
        for z in range(1, zs):
            total += got_ref[source * zs + z].astype(F32)
        out_ref[0, place * share : (place + 1) * share, :] = total


def collect(got, teams):
    share, trials = got.shape[1:]
    return pl.pallas_call(
        functools.partial(collect_kernel, teams),
        out_shape=jax.ShapeDtypeStruct((1, teams * share, trials), F32),
        in_specs=[WHOLE],
        out_specs=WHOLE,
        compiler_params=pltpu.CompilerParams(vmem_limit_bytes=SMALL),
    )(got)


def pairs_of(teams, zs, along_x):
    pairs = []
    for tm in range(teams):
        for z in range(zs):
            for xl in range(2):
                if along_x:
                    to = tm ^ 2 if tm & 1 else tm, z, 1 - xl
                else:
                    to = tm, ((z - 1 + 2 * (z & 1)) % zs if tm & 1 else z ^ 1), xl
                pairs.append(((tm * zs + z) * 2 + xl, (to[0] * zs + to[1]) * 2 + to[2]))
    return pairs


def body(
    occ_rows,
    emp_rows,
    occ_cols,
    emp_cols,
    occ_energy,
    emp_energy,
    time_points,
    time_weights,
    frequencies,
    trial_vectors,
):
    teams, zs = lax.axis_size("tm"), 2 * lax.axis_size("zh")
    share = occ_rows.shape[1] // teams

    sent, factor = pick(
        time_points,
        occ_energy,
        emp_energy,
        occ_rows.T,
        emp_rows.T,
        2 * zs,
        share,
    )
    rows = lax.all_to_all(sent, COL, split_axis=0, concat_axis=0, tiled=True)

    x_pairs, z_pairs = pairs_of(teams, zs, True), pairs_of(teams, zs, False)
    with jax.named_scope("for_both"):
        both, high, low = first_products(
            3, rows, factor, occ_cols, emp_cols, trial_vectors, share
        )
    held = (rows, factor, occ_cols, emp_cols, high, low, share)
    with jax.named_scope("x_first"):
        from_x = lax.ppermute(both, ALL, x_pairs)
    with jax.named_scope("for_x"):
        along_x = next_products(1, *held, BF16)
    with jax.named_scope("x_second"):
        own_from_x = lax.ppermute(along_x, ALL, x_pairs)
    with jax.named_scope("for_z"):
        along_z = next_products(2, *held, F32)
    with jax.named_scope("z_only"):
        from_z = lax.ppermute((along_z + from_x.astype(F32)).astype(BF16), ALL, z_pairs)
    with jax.named_scope("for_own"):
        grid = tuple(map(far_ref, (time_points, time_weights, frequencies)))
        own, spread = next_products(0, *held, F32, grid)
    sent = mix(spread, own, own_from_x, from_z, share)
    got = lax.all_to_all(sent, ("tm", "zh"), split_axis=0, concat_axis=0, tiled=True)
    return collect(got, teams)


def solution(mesh):
    torus = Mesh(mesh.devices.reshape(mesh.shape["tm"], mesh.shape["col"] // 4, 2, 2), ALL)
    in_specs = (
        P(None, COL),
        P(None, COL),
        P(None, COL),
        P(None, COL),
        P(),
        P(),
        P(),
        P(),
        P(),
        P(COL, None),
    )
    out_specs = P("tm", COL, None)
    return jax.shard_map(body, mesh=torus, in_specs=in_specs, out_specs=out_specs, check_vma=False)
```

time: 156 us -> 63.3 us (0.41)
  waiting for transfers between devices: 80.5 us -> 3.9 us
  matrix products: 14.9 us -> 0 us
  between operations: 13.5 us -> 0.07 us
  blocking collectives: 34.8 us -> 45.6 us
  Pallas kernels: 0 us -> 10.5 us
  other arithmetic: 5.01 us -> 0.07 us
  starting transfers between devices: 5.18 us -> 2.94 us
  local copies, waits for them, and re-layouts: 1.91 us -> 0.01 us
    all_gather x1 -> x0, waiting for transfers between devices: 57.3 us -> none  [gathered_by_axis(): value = lax.all_gather(value, axis, axis=dim, tiled=True)]
    all_to_all x1 -> x0, waiting for transfers between devices: 23.3 us -> none  [sum_at_owner(): lax.all_to_all(parts, axis, split_axis=0, concat_axis=0, tiled=True)]
    all_to_all x1 -> x2, blocking collectives: 27.3 us -> 45.6 us  [the longest x1 25.1 us: body(): lax.all_to_all(sent, ('tm', 'zh'), split_axis=0, concat_axis=0, tiled=True)]
    dot_general x3 -> x0, matrix products: 14.9 us -> none  [the longest x1 7.67 us: body(): jnp.dot(polar, trial_vectors, precision=lax.Precision.HIGHEST, preferred_...]
    pallas_call x0 -> x7, Pallas kernels: none -> 10.5 us  [the longest x3 6.16 us: next_products(): pl.pallas_call(functools.partial(table_kernel if grid else next_kernel, s...]
    all_gather x1 -> x0, blocking collectives: 7.48 us -> none  [gathered_by_axis(): value = lax.all_gather(value, axis, axis=dim, tiled=True)]
    all_to_all x1 -> x0, starting transfers between devices: 5.18 us -> none  [sum_at_owner(): lax.all_to_all(parts, axis, split_axis=0, concat_axis=0, tiled=True)]
    ppermute x0 -> x3, waiting for transfers between devices: none -> 3.9 us  [the longest x1 3.24 us: body(): lax.ppermute((along_z + from_x.astype(F32)).astype(BF16), ALL, z_pairs)]
  transfers between devices with their start and end apart: 2 -> 3, of which waited for: 2 -> 3; matrix products, arithmetic and copies ran while one was open for 3% -> 0% of each run, Pallas kernels for 0% -> 10%
where the time goes in v4:
time: 63.3 us; the launch traced here: 63.1 us
  blocking collectives  45.6 us (72%)
  Pallas kernels  10.5 us (17%)
  waiting for transfers between devices  3.9 us (6%)
  starting transfers between devices  2.94 us (5%)
    all_to_all x1, blocking collectives, body(): lax.all_to_all(sent, ('tm', 'zh'), split_axis=0, concat_axis=0, tiled=True)  25.1 us
    all_to_all x1, blocking collectives, body(): rows = lax.all_to_all(sent, COL, split_axis=0, concat_axis=0, tiled=True)  20.5 us
    pallas_call x3, Pallas kernels, next_products(): pl.pallas_call(functools.partial(table_kernel if grid else next_kernel, s...  6.16 us
    ppermute x1, waiting for transfers between devices, body(): lax.ppermute((along_z + from_x.astype(F32)).astype(BF16), ALL, z_pairs)  3.24 us
    pallas_call x1, Pallas kernels, first_products(): pl.pallas_call(functools.partial(first_kernel, share, part), out_shape=(j...  1.84 us
    ppermute x1, starting transfers between devices, body(): from_x = lax.ppermute(both, ALL, x_pairs)  1.56 us
    pallas_call x1, Pallas kernels, pick(): pl.pallas_call(functools.partial(pick_kernel, share), out_shape=(jax.Shap...  1.36 us
    ppermute x1, starting transfers between devices, body(): own_from_x = lax.ppermute(along_x, ALL, x_pairs)  1.29 us
  transfers between devices with their start and end apart: 3, of which 3 were waited for; matrix products, arithmetic and copies ran while one was open for 0% of the time, Pallas kernels for 10%

profile of v4, /device:TPU:1, one launch (start us, length us, event | category | flops | bytes accessed | tf_op | source)
XLA Modules:
  0.0 63.1 jit_solution(11513325695292893150)
XLA Ops:
  0.0 0.0 copy-start
  0.0 0.0 copy-start.1
  0.0 0.0 copy-start.2
  0.0 1.4 %shard_map.100 = (bf16[16,8,1024]{2,1,0:T(8,128)(2,1)S(1)}, f32[2,16,1024]{2,1,0:T(8,128)S(1)}) custom-call(f32[1,16]{1,0:T(1,128)} %bitcast.5, f32[1,1024]{1,0:T(1,128)} %bitcast.8, f32[1,1024]{1,0:T(1,128)} %bitcast.9, bf16[64,1024]{1,0:T(8,128)(2,1)} %bitcast.6, bf16[64,1024]{1,0:T(8,128)(2,1)} %bitcast.7), custom_call_target="tpu_custom_call" | custom-call | flops 34359738368 | bytes 1048576 | tf_op jit(solution)/shard_map/pallas_call | solution.py:79
  1.4 20.5 %all_to_all.10.rows_ref.refs_0_ = bf16[16,8,1024]{2,1,0:T(8,128)(2,1)S(1)} all-to-all(bf16[16,8,1024]{2,1,0:T(8,128)(2,1)S(1)} %get-tuple-element.12), channel_id=1, replica_groups=mesh['tm'=16,'zh'=4,'zl'=2,'xl'=2] {'zh','zl','xl'}, dimensions={0} | all-to-all | bytes 524288 | tf_op jit(solution)/shard_map/all_to_all | solution.py:302
  21.9 0.0 copy-done
  21.9 0.0 copy-done.1
  21.9 0.0 copy-done.2
  21.9 1.8 %for_both.1 = (bf16[256,512]{1,0:T(8,128)(2,1)S(1)}, bf16[1024,512]{1,0:T(8,128)(2,1)S(1)}, bf16[1024,512]{1,0:T(8,128)(2,1)S(1)}) custom-call(bf16[16,8,1024]{2,1,0:T(8,128)(2,1)S(1)} %all_to_all.10.rows_ref.refs_0_, f32[2,16,1024]{2,1,0:T(8,128)S(1)} %get-tuple-element.13.factor_ref.refs_1_, bf16[1024,1024]{1,0:T(8,128)(2,1)S(1)} %copy-done, ...), custom_call_target="tpu_custom_call" | custom-call | flops 1610612736 | bytes 8388608 | tf_op jit(solution)/shard_map/for_both/pallas_call | solution.py:188
  23.8 1.6 %collective-permute-start.1 = (bf16[256,512]{1,0:T(8,128)(2,1)S(1)}, bf16[256,512]{1,0:T(8,128)(2,1)S(1)}, u32[]{:S(2)}, u32[]{:S(2)}) collective-permute-start(bf16[256,512]{1,0:T(8,128)(2,1)S(1)} %get-tuple-element.18), channel_id=1, source_target_pairs={{0,1},{1,0},{2,3},{3,2},{4,5},{5,4},{6,7},{7,6},{8,9},{9,8},{10,11... | collective-permute-start | bytes 786440 | tf_op jit(solution)/shard_map/x_first/ppermute | solution.py:311
  25.3 1.8 %for_x.1 = bf16[256,512]{1,0:T(8,128)(2,1)S(1)} custom-call(bf16[16,8,1024]{2,1,0:T(8,128)(2,1)S(1)} %all_to_all.10.rows_ref.refs_0_, f32[2,16,1024]{2,1,0:T(8,128)S(1)} %get-tuple-element.13.factor_ref.refs_1_, bf16[1024,1024]{1,0:T(8,128)(2,1)S(1)} %copy-done, bf16[1024,1024]{1,0:T(8,128)(2,1)S(1)} %copy-done.1, ...), custom_call_target="tpu_custom_call" | custom-call | flops 1610612736 | bytes 8388608 | tf_op jit(solution)/shard_map/for_x/pallas_call | solution.py:209
  27.1 1.3 %collective-permute-start = (bf16[256,512]{1,0:T(8,128)(2,1)S(1)}, bf16[256,512]{1,0:T(8,128)(2,1)S(1)}, u32[]{:S(2)}, u32[]{:S(2)}) collective-permute-start(bf16[256,512]{1,0:T(8,128)(2,1)S(1)} %for_x.1), channel_id=1, source_target_pairs={{0,1},{1,0},{2,3},{3,2},{4,5},{5,4},{6,7},{7,6},{8,9},{9,8},{10,11... | collective-permute-start | bytes 786440 | tf_op jit(solution)/shard_map/x_second/ppermute | solution.py:315
  28.4 1.8 %for_z.1 = f32[256,512]{1,0:T(8,128)S(1)} custom-call(bf16[16,8,1024]{2,1,0:T(8,128)(2,1)S(1)} %all_to_all.10.rows_ref.refs_0_, f32[2,16,1024]{2,1,0:T(8,128)S(1)} %get-tuple-element.13.factor_ref.refs_1_, bf16[1024,1024]{1,0:T(8,128)(2,1)S(1)} %copy-done, bf16[1024,1024]{1,0:T(8,128)(2,1)S(1)} %copy-done.1, ...), custom_call_target="tpu_custom_call" | custom-call | flops 1610612736 | bytes 8388608 | tf_op jit(solution)/shard_map/for_z/pallas_call | solution.py:209
  30.2 0.1 collective-permute-done.1
  30.3 0.1 add_convert_fusion
  30.4 0.1 collective-permute-start.2
  30.5 2.6 %for_own.1 = (f32[256,512]{1,0:T(8,128)S(1)}, bf16[2,256,256]{2,1,0:T(8,128)(2,1)S(1)}) custom-call(f32[16]{0:T(128)} %times_ref.1, f32[16]{0:T(128)} %weights_ref.1, f32[16]{0:T(128)} %freqs_ref.1, bf16[16,8,1024]{2,1,0:T(8,128)(2,1)S(1)} %all_to_all.10.rows_ref.refs_0_, f32[2,16,1024]{2,1,0:T(8,128)S(1)} %get-tuple-element.13.factor_ref.refs_1_, ...), custom_call_target="tpu_custom_call" | custom-call | flops 1610612736 | bytes 8388608 | tf_op jit(solution)/shard_map/for_own/pallas_call | solution.py:209
  33.1 0.6 collective-permute-done.x_ref
  33.7 3.2 %collective-permute-done.2.z_ref = bf16[256,512]{1,0:T(8,128)(2,1)S(1)} collective-permute-done((bf16[256,512]{1,0:T(8,128)(2,1)S(1)}, bf16[256,512]{1,0:T(8,128)(2,1)S(1)}, u32[]{:S(2)}, u32[]{:S(2)}) %collective-permute-start.2) | collective-permute-done | bytes 262176 | tf_op jit(solution)/shard_map/z_only/ppermute | solution.py:319
  36.9 0.4 shard_map.101
  37.3 25.1 %all_to_all.11.got_ref = bf16[64,4,512]{2,1,0:T(4,128)(2,1)S(1)} all-to-all(bf16[64,4,512]{2,1,0:T(4,128)(2,1)S(1)} %shard_map.101), channel_id=1, replica_groups=mesh['tm'=16,'zh'=4,'zl'=2,'xl'=2] {'tm','zh'}, dimensions={0} | all-to-all | bytes 524288 | tf_op jit(solution)/shard_map/all_to_all | solution.py:324
  62.4 0.7 %shard_map.102 = f32[1,64,512]{2,1,0:T(8,128)} custom-call(bf16[64,4,512]{2,1,0:T(4,128)(2,1)S(1)} %all_to_all.11.got_ref), custom_call_target="tpu_custom_call" | custom-call | tf_op jit(solution)/shard_map/pallas_call | solution.py:256
Async XLA Ops:
  0.0 21.9 %copy-start = (bf16[1024,1024]{1,0:T(8,128)(2,1)S(1)}, bf16[1024,1024]{1,0:T(8,128)(2,1)}, u32[]{:S(2)}) copy-start(bf16[1024,1024]{1,0:T(8,128)(2,1)} %occ_ref.5) | copy-start | bytes 6291460
  0.0 21.9 %copy-start.1 = (bf16[1024,1024]{1,0:T(8,128)(2,1)S(1)}, bf16[1024,1024]{1,0:T(8,128)(2,1)}, u32[]{:S(2)}) copy-start(bf16[1024,1024]{1,0:T(8,128)(2,1)} %emp_ref.5) | copy-start | bytes 6291460
  0.0 21.9 %copy-start.2 = (f32[1024,512]{1,0:T(8,128)S(1)}, f32[1024,512]{1,0:T(8,128)}, u32[]{:S(2)}) copy-start(f32[1024,512]{1,0:T(8,128)} %trial_ref.1) | copy-start | bytes 6291460
  23.8 6.5 %collective-permute-start.1 = (bf16[256,512]{1,0:T(8,128)(2,1)S(1)}, bf16[256,512]{1,0:T(8,128)(2,1)S(1)}, u32[]{:S(2)}, u32[]{:S(2)}) collective-permute-start(bf16[256,512]{1,0:T(8,128)(2,1)S(1)} %get-tuple-element.18), channel_id=1, source_target_pairs={{0,1},{1,0},{2,3},{3,2},{4,5},{5,4},{6,7},{7,6},{8,9},{9,8},{10,11... | collective-permute-start | bytes 786440 | tf_op jit(solution)/shard_map/x_first/ppermute | solution.py:311
  27.1 6.5 %collective-permute-start = (bf16[256,512]{1,0:T(8,128)(2,1)S(1)}, bf16[256,512]{1,0:T(8,128)(2,1)S(1)}, u32[]{:S(2)}, u32[]{:S(2)}) collective-permute-start(bf16[256,512]{1,0:T(8,128)(2,1)S(1)} %for_x.1), channel_id=1, source_target_pairs={{0,1},{1,0},{2,3},{3,2},{4,5},{5,4},{6,7},{7,6},{8,9},{9,8},{10,11... | collective-permute-start | bytes 786440 | tf_op jit(solution)/shard_map/x_second/ppermute | solution.py:315
  30.4 6.5 %collective-permute-start.2 = (bf16[256,512]{1,0:T(8,128)(2,1)S(1)}, bf16[256,512]{1,0:T(8,128)(2,1)S(1)}, u32[]{:S(2)}, u32[]{:S(2)}) collective-permute-start(bf16[256,512]{1,0:T(8,128)(2,1)S(1)} %add_convert_fusion), channel_id=1, source_target_pairs={{0,2},{1,3},{2,0},{3,1},{4,6},{5,7},{6,4},{7,5},{8,10},{9,11},{10,... | collective-permute-start | bytes 786440 | tf_op jit(solution)/shard_map/z_only/ppermute | solution.py:319

commit v5 on v4

--- a/solution.py
+++ b/solution.py
@@ -16,6 +16,7 @@
 SMALL, LARGE = 12 << 20, 20 << 20
 BLOCK = 4
 PICKCOST = 1 << 35
+FIRST = 2
 
 
 def far_ref(value):
@@ -217,37 +218,50 @@
     )(*grid, rows, factor, occ_cols, emp_cols, high, low)
 
 
-def mix_kernel(share, spread_ref, own_ref, x_ref, z_ref, out_ref):
-    total = own_ref[...] + x_ref[...].astype(F32) + z_ref[...].astype(F32)
+def last_order(members, zs):
+    teams = range(members // zs)
+    return [t * zs + z for z in range(zs)[::-1] for t in teams[::-1]]
+
+
+def mix_kernel(share, spread_ref, own_ref, *refs):
+    *parts, out_ref = refs
+    total = own_ref[...]
+    for part in parts:
+        total += part[...].astype(F32)
     main, rest = halves(total)
     mixed = jnp.dot(spread_ref[0], rest, preferred_element_type=F32)
     mixed += jnp.dot(spread_ref[1], main, preferred_element_type=F32)
     mixed += jnp.dot(spread_ref[0], main, preferred_element_type=F32)
     mixed = mixed.astype(BF16)
-    for place in range(out_ref.shape[0]):
-        out_ref[place] = mixed[place * share : (place + 1) * share, :]
-
-
-def mix(spread, own, from_x, from_z, share):
+    for place, member in enumerate(last_order(out_ref.shape[0], BLOCK)):
+        out_ref[place] = mixed[member * share : (member + 1) * share, :]
+
+
+def mix(spread, own, *rest):
+    *parts, share = rest
     lines, trials = own.shape
     return pl.pallas_call(
         functools.partial(mix_kernel, share),
         out_shape=jax.ShapeDtypeStruct((lines // share, share, trials), BF16),
-        in_specs=[WHOLE] * 4,
+        in_specs=[WHOLE] * (2 + len(parts)),
         out_specs=WHOLE,
         compiler_params=pltpu.CompilerParams(vmem_limit_bytes=SMALL),
-    )(spread, own, from_x, from_z)
+    )(spread, own, *parts)
 
 
 def collect_kernel(teams, got_ref, out_ref):
     share = got_ref.shape[1]
     zs = got_ref.shape[0] // teams
-    turn = 2 * lax.axis_index("xl")
+    turn = lax.axis_index("xl")
+    order = last_order(got_ref.shape[0], zs)
     for place in range(teams):
-        source = place ^ turn if place & 1 else place
-        total = got_ref[source * zs].astype(F32)
-        for z in range(1, zs):
-            total += got_ref[source * zs + z].astype(F32)
+        total = None
+        for z in range(zs):
+            slot = order.index(place * zs + z)
+            if place & 1:
+                slot = jnp.where(turn == 0, slot, order.index((place ^ 2) * zs + z))
+            part = got_ref[slot].astype(F32)
+            total = part if total is None else total + part
         out_ref[0, place * share : (place + 1) * share, :] = total
 
 
@@ -262,16 +276,17 @@
     )(got)
 
 
-def pairs_of(teams, zs, along_x):
+def pairs_of(teams, zs, along_x, along_z):
     pairs = []
     for tm in range(teams):
         for z in range(zs):
             for xl in range(2):
-                if along_x:
-                    to = tm ^ 2 if tm & 1 else tm, z, 1 - xl
-                else:
-                    to = tm, ((z - 1 + 2 * (z & 1)) % zs if tm & 1 else z ^ 1), xl
-                pairs.append(((tm * zs + z) * 2 + xl, (to[0] * zs + to[1]) * 2 + to[2]))
+                team, to = tm, z
+                if along_x and tm & 1:
+                    team = tm ^ 2
+                if along_z:
+                    to = (z - 1 + 2 * (z & 1)) % zs if tm & 1 else z ^ 1
+                pairs.append(((tm * zs + z) * 2 + xl, (team * zs + to) * 2 + (xl ^ along_x)))
     return pairs
 
 
@@ -301,27 +316,24 @@
     )
     rows = lax.all_to_all(sent, COL, split_axis=0, concat_axis=0, tiled=True)
 
-    x_pairs, z_pairs = pairs_of(teams, zs, True), pairs_of(teams, zs, False)
-    with jax.named_scope("for_both"):
-        both, high, low = first_products(
-            3, rows, factor, occ_cols, emp_cols, trial_vectors, share
-        )
+    both, high, low = first_products(3, rows, factor, occ_cols, emp_cols, trial_vectors, share)
     held = (rows, factor, occ_cols, emp_cols, high, low, share)
-    with jax.named_scope("x_first"):
-        from_x = lax.ppermute(both, ALL, x_pairs)
-    with jax.named_scope("for_x"):
-        along_x = next_products(1, *held, BF16)
-    with jax.named_scope("x_second"):
-        own_from_x = lax.ppermute(along_x, ALL, x_pairs)
-    with jax.named_scope("for_z"):
-        along_z = next_products(2, *held, F32)
-    with jax.named_scope("z_only"):
-        from_z = lax.ppermute((along_z + from_x.astype(F32)).astype(BF16), ALL, z_pairs)
-    with jax.named_scope("for_own"):
-        grid = tuple(map(far_ref, (time_points, time_weights, frequencies)))
-        own, spread = next_products(0, *held, F32, grid)
-    sent = mix(spread, own, own_from_x, from_z, share)
-    got = lax.all_to_all(sent, ("tm", "zh"), split_axis=0, concat_axis=0, tiled=True)
+    from_both = lax.ppermute(both, ALL, pairs_of(teams, zs, 1, 1))
+    first = next_products(FIRST, *held, BF16)
+    from_first = lax.ppermute(first, ALL, pairs_of(teams, zs, FIRST & 1, FIRST >> 1))
+    second = next_products(3 - FIRST, *held, BF16)
+    from_second = lax.ppermute(second, ALL, pairs_of(teams, zs, 1 - (FIRST & 1), 1 - (FIRST >> 1)))
+    grid = tuple(map(far_ref, (time_points, time_weights, frequencies)))
+    own, spread = next_products(0, *held, F32, grid)
+    sent = mix(spread, own, from_both, from_first, from_second, share)
+    got = lax.all_to_all(
+        sent,
+        ("tm", "zh"),
+        split_axis=0,
+        concat_axis=0,
+        axis_index_groups=[last_order(sent.shape[0], zs // 2)],
+        tiled=True,
+    )
     return collect(got, teams)
 
 

time: 63.3 us -> 61.3 us (0.968)
  blocking collectives: 45.6 us -> 42.9 us
  starting transfers between devices: 2.94 us -> 5.23 us
  waiting for transfers between devices: 3.9 us -> 2.35 us
    all_to_all x1, blocking collectives: 25.1 us -> 22.4 us  [body(): lax.all_to_all(sent, ('tm', 'zh'), split_axis=0, concat_axis=0, axis_inde...]
    ppermute x3, starting transfers between devices: 2.94 us -> 5.23 us  [the longest x1 3.58 us: body(): from_both = lax.ppermute(both, ALL, pairs_of(teams, zs, 1, 1))]
    ppermute x3, waiting for transfers between devices: 3.9 us -> 2.35 us  [the longest x1 2.34 us: body(): from_both = lax.ppermute(both, ALL, pairs_of(teams, zs, 1, 1))]
  transfers between devices with their start and end apart: 3 -> 3, of which waited for: 3 -> 1; matrix products, arithmetic and copies ran while one was open for 0% -> 0% of each run, Pallas kernels for 10% -> 7%
where the time goes in v5:
time: 61.3 us; the launch traced here: 61.1 us
  blocking collectives  42.9 us (70%)
  Pallas kernels  10.5 us (17%)
  starting transfers between devices  5.23 us (9%)
  waiting for transfers between devices  2.35 us (4%)
    all_to_all x1, blocking collectives, body(): lax.all_to_all(sent, ('tm', 'zh'), split_axis=0, concat_axis=0, axis_inde...  22.4 us
    all_to_all x1, blocking collectives, body(): rows = lax.all_to_all(sent, COL, split_axis=0, concat_axis=0, tiled=True)  20.5 us
    pallas_call x3, Pallas kernels, next_products(): pl.pallas_call(functools.partial(table_kernel if grid else next_kernel, s...  6.17 us
    ppermute x1, starting transfers between devices, body(): from_both = lax.ppermute(both, ALL, pairs_of(teams, zs, 1, 1))  3.58 us
    ppermute x1, waiting for transfers between devices, body(): from_both = lax.ppermute(both, ALL, pairs_of(teams, zs, 1, 1))  2.34 us
    pallas_call x1, Pallas kernels, first_products(): pl.pallas_call(functools.partial(first_kernel, share, part), out_shape=(j...  1.84 us
    ppermute x1, starting transfers between devices, body(): lax.ppermute(second, ALL, pairs_of(teams, zs, 1 - (FIRST & 1), 1 - (FIRST...  1.56 us
    pallas_call x1, Pallas kernels, pick(): pl.pallas_call(functools.partial(pick_kernel, share), out_shape=(jax.Shap...  1.36 us
  transfers between devices with their start and end apart: 3, of which 1 were waited for; matrix products, arithmetic and copies ran while one was open for 0% of the time, Pallas kernels for 7%

profile of v5, /device:TPU:1, one launch (start us, length us, event | category | flops | bytes accessed | tf_op | source)
XLA Modules:
  0.0 61.1 jit_solution(14050109422757367260)
XLA Ops:
  0.0 0.0 copy-start
  0.0 0.0 copy-start.1
  0.0 0.0 copy-start.2
  0.0 1.4 %shard_map.100 = (bf16[16,8,1024]{2,1,0:T(8,128)(2,1)S(1)}, f32[2,16,1024]{2,1,0:T(8,128)S(1)}) custom-call(f32[1,16]{1,0:T(1,128)} %bitcast.5, f32[1,1024]{1,0:T(1,128)} %bitcast.8, f32[1,1024]{1,0:T(1,128)} %bitcast.9, bf16[64,1024]{1,0:T(8,128)(2,1)} %bitcast.6, bf16[64,1024]{1,0:T(8,128)(2,1)} %bitcast.7), custom_call_target="tpu_custom_call" | custom-call | flops 34359738368 | bytes 1048576 | tf_op jit(solution)/shard_map/pallas_call | solution.py:80
  1.4 20.5 %all_to_all.10.rows_ref.refs_0_ = bf16[16,8,1024]{2,1,0:T(8,128)(2,1)S(1)} all-to-all(bf16[16,8,1024]{2,1,0:T(8,128)(2,1)S(1)} %get-tuple-element.12), channel_id=1, replica_groups=mesh['tm'=16,'zh'=4,'zl'=2,'xl'=2] {'zh','zl','xl'}, dimensions={0} | all-to-all | bytes 524288 | tf_op jit(solution)/shard_map/all_to_all | solution.py:317
  21.9 0.0 copy-done
  21.9 0.0 copy-done.1
  21.9 0.0 copy-done.2
  21.9 1.8 %shard_map.101 = (bf16[256,512]{1,0:T(8,128)(2,1)S(1)}, bf16[1024,512]{1,0:T(8,128)(2,1)S(1)}, bf16[1024,512]{1,0:T(8,128)(2,1)S(1)}) custom-call(bf16[16,8,1024]{2,1,0:T(8,128)(2,1)S(1)} %all_to_all.10.rows_ref.refs_0_, f32[2,16,1024]{2,1,0:T(8,128)S(1)} %get-tuple-element.13.factor_ref.refs_1_, bf16[1024,1024]{1,0:T(8,128)(2,1)S(1)} %copy-done, ...), custom_call_target="tpu_custom_call" | custom-call | flops 1610612736 | bytes 8388608 | tf_op jit(solution)/shard_map/pallas_call | solution.py:189
  23.8 1.8 %shard_map.103 = bf16[256,512]{1,0:T(8,128)(2,1)S(1)} custom-call(bf16[16,8,1024]{2,1,0:T(8,128)(2,1)S(1)} %all_to_all.10.rows_ref.refs_0_, f32[2,16,1024]{2,1,0:T(8,128)S(1)} %get-tuple-element.13.factor_ref.refs_1_, bf16[1024,1024]{1,0:T(8,128)(2,1)S(1)} %copy-done, bf16[1024,1024]{1,0:T(8,128)(2,1)S(1)} %copy-done.1, ...), custom_call_target="tpu_custom_call" | custom-call | flops 1610612736 | bytes 8388608 | tf_op jit(solution)/shard_map/pallas_call | solution.py:210
  25.6 0.1 collective-permute-start.1
  25.7 1.8 %shard_map.104 = bf16[256,512]{1,0:T(8,128)(2,1)S(1)} custom-call(bf16[16,8,1024]{2,1,0:T(8,128)(2,1)S(1)} %all_to_all.10.rows_ref.refs_0_, f32[2,16,1024]{2,1,0:T(8,128)S(1)} %get-tuple-element.13.factor_ref.refs_1_, bf16[1024,1024]{1,0:T(8,128)(2,1)S(1)} %copy-done, bf16[1024,1024]{1,0:T(8,128)(2,1)S(1)} %copy-done.1, ...), custom_call_target="tpu_custom_call" | custom-call | flops 1610612736 | bytes 8388608 | tf_op jit(solution)/shard_map/pallas_call | solution.py:210
  27.5 1.6 %collective-permute-start.2 = (bf16[256,512]{1,0:T(8,128)(2,1)S(1)}, bf16[256,512]{1,0:T(8,128)(2,1)S(1)}, u32[]{:S(2)}, u32[]{:S(2)}) collective-permute-start(bf16[256,512]{1,0:T(8,128)(2,1)S(1)} %shard_map.104), channel_id=1, source_target_pairs={{0,1},{1,0},{2,3},{3,2},{4,5},{5,4},{6,7},{7,6},{8,9},{9,8},{10,11... | collective-permute-start | bytes 786440 | tf_op jit(solution)/shard_map/ppermute | solution.py:325
  29.0 3.6 %collective-permute-start = (bf16[256,512]{1,0:T(8,128)(2,1)S(1)}, bf16[256,512]{1,0:T(8,128)(2,1)S(1)}, u32[]{:S(2)}, u32[]{:S(2)}) collective-permute-start(bf16[256,512]{1,0:T(8,128)(2,1)S(1)} %get-tuple-element.18), channel_id=1, source_target_pairs={{0,3},{1,2},{2,1},{3,0},{4,7},{5,6},{6,5},{7,4},{8,11},{9,10},{10,... | collective-permute-start | bytes 786440 | tf_op jit(solution)/shard_map/ppermute | solution.py:321
  32.6 2.6 %shard_map.102 = (f32[256,512]{1,0:T(8,128)S(1)}, bf16[2,256,256]{2,1,0:T(8,128)(2,1)S(1)}) custom-call(f32[16]{0:T(128)} %times_ref.1, f32[16]{0:T(128)} %weights_ref.1, f32[16]{0:T(128)} %freqs_ref.1, bf16[16,8,1024]{2,1,0:T(8,128)(2,1)S(1)} %all_to_all.10.rows_ref.refs_0_, f32[2,16,1024]{2,1,0:T(8,128)S(1)} %get-tuple-element.13.factor_ref.refs_1_, ...), custom_call_target="tpu_custom_call" | custom-call | flops 1610612736 | bytes 8388608 | tf_op jit(solution)/shard_map/pallas_call | solution.py:210
  35.2 0.0 collective-permute-done.1.refs_1_
  35.2 0.0 collective-permute-done.2.refs_2_
  35.2 2.3 %collective-permute-done.refs_0_ = bf16[256,512]{1,0:T(8,128)(2,1)S(1)} collective-permute-done((bf16[256,512]{1,0:T(8,128)(2,1)S(1)}, bf16[256,512]{1,0:T(8,128)(2,1)S(1)}, u32[]{:S(2)}, u32[]{:S(2)}) %collective-permute-start) | collective-permute-done | bytes 262176 | tf_op jit(solution)/shard_map/ppermute | solution.py:321
  37.6 0.4 shard_map.105
  38.0 22.4 %all_to_all.11.got_ref = bf16[64,4,512]{2,1,0:T(4,128)(2,1)S(1)} all-to-all(bf16[64,4,512]{2,1,0:T(4,128)(2,1)S(1)} %shard_map.105), channel_id=1, replica_groups={{252,236,220,204,188,172,156,140,124,108,92,76,60,44,28,12,248,232,216,..., dimensions={0} | all-to-all | bytes 524288 | tf_op jit(solution)/shard_map/all_to_all | solution.py:329
  60.4 0.7 %shard_map.106 = f32[1,64,512]{2,1,0:T(8,128)} custom-call(bf16[64,4,512]{2,1,0:T(4,128)(2,1)S(1)} %all_to_all.11.got_ref), custom_call_target="tpu_custom_call" | custom-call | tf_op jit(solution)/shard_map/pallas_call | solution.py:270
Async XLA Ops:
  0.0 21.9 %copy-start = (bf16[1024,1024]{1,0:T(8,128)(2,1)S(1)}, bf16[1024,1024]{1,0:T(8,128)(2,1)}, u32[]{:S(2)}) copy-start(bf16[1024,1024]{1,0:T(8,128)(2,1)} %occ_ref.5) | copy-start | bytes 6291460
  0.0 21.9 %copy-start.1 = (bf16[1024,1024]{1,0:T(8,128)(2,1)S(1)}, bf16[1024,1024]{1,0:T(8,128)(2,1)}, u32[]{:S(2)}) copy-start(bf16[1024,1024]{1,0:T(8,128)(2,1)} %emp_ref.5) | copy-start | bytes 6291460
  0.0 21.9 %copy-start.2 = (f32[1024,512]{1,0:T(8,128)S(1)}, f32[1024,512]{1,0:T(8,128)}, u32[]{:S(2)}) copy-start(f32[1024,512]{1,0:T(8,128)} %trial_ref.1) | copy-start | bytes 6291460
  25.6 9.6 %collective-permute-start.1 = (bf16[256,512]{1,0:T(8,128)(2,1)S(1)}, bf16[256,512]{1,0:T(8,128)(2,1)S(1)}, u32[]{:S(2)}, u32[]{:S(2)}) collective-permute-start(bf16[256,512]{1,0:T(8,128)(2,1)S(1)} %shard_map.103), channel_id=1, source_target_pairs={{0,2},{1,3},{2,0},{3,1},{4,6},{5,7},{6,4},{7,5},{8,10},{9,11},{10,... | collective-permute-start | bytes 786440 | tf_op jit(solution)/shard_map/ppermute | solution.py:323
  27.5 7.7 %collective-permute-start.2 = (bf16[256,512]{1,0:T(8,128)(2,1)S(1)}, bf16[256,512]{1,0:T(8,128)(2,1)S(1)}, u32[]{:S(2)}, u32[]{:S(2)}) collective-permute-start(bf16[256,512]{1,0:T(8,128)(2,1)S(1)} %shard_map.104), channel_id=1, source_target_pairs={{0,1},{1,0},{2,3},{3,2},{4,5},{5,4},{6,7},{7,6},{8,9},{9,8},{10,11... | collective-permute-start | bytes 786440 | tf_op jit(solution)/shard_map/ppermute | solution.py:325
  29.0 8.5 %collective-permute-start = (bf16[256,512]{1,0:T(8,128)(2,1)S(1)}, bf16[256,512]{1,0:T(8,128)(2,1)S(1)}, u32[]{:S(2)}, u32[]{:S(2)}) collective-permute-start(bf16[256,512]{1,0:T(8,128)(2,1)S(1)} %get-tuple-element.18), channel_id=1, source_target_pairs={{0,3},{1,2},{2,1},{3,0},{4,7},{5,6},{6,5},{7,4},{8,11},{9,10},{10,... | collective-permute-start | bytes 786440 | tf_op jit(solution)/shard_map/ppermute | solution.py:321

commit v6 on v5

--- a/solution.py
+++ b/solution.py
@@ -21,6 +21,11 @@
 
 def far_ref(value):
     return pltpu.with_memory_space_constraint(value, pltpu.HBM)
+
+
+def ring_order(peers):
+    zs = range(peers // 2)
+    return [2 * (-z % len(zs)) + xl for xl in range(2) for z in zs]
 
 
 def pick_kernel(
@@ -61,8 +66,9 @@
         both = jnp.dot(occ_pick, held[2 * side], preferred_element_type=F32)
         both += jnp.dot(emp_pick.astype(BF16), held[2 * side + 1], preferred_element_type=F32)
         both = both.astype(BF16)
-        for peer in range(side, out_ref.shape[0], 2):
-            out_ref[peer] = both
+        for place, peer in enumerate(ring_order(out_ref.shape[0])):
+            if peer % 2 == side:
+                out_ref[place] = both
     for copy in copies[4:7]:
         copy.wait()
     times = times_ref.shape[1]
@@ -110,9 +116,13 @@
 def scale(share, part, rows_ref, factor_ref, scaled):
     times = factor_ref.shape[1]
     occ_s, emp_s = scaled
-    start = 2 * (lax.axis_index("zl") ^ (part >> 1)) + (lax.axis_index("xl") ^ (part & 1))
+    kind = 2 * (lax.axis_index("zl") ^ (part >> 1)) + (lax.axis_index("xl") ^ (part & 1))
+    order = ring_order(rows_ref.shape[0])
     for index in range(BLOCK):
-        rows = rows_ref[4 * index + start].astype(F32)
+        slot = order.index(4 * index)
+        for other in range(1, 4):
+            slot = jnp.where(kind == other, order.index(4 * index + other), slot)
+        rows = rows_ref[slot].astype(F32)
         for r in range(share):
             at = (index * share + r) * times
             occ_s[at : at + times, :] = (rows[r : r + 1, :] * factor_ref[0]).astype(BF16)
@@ -220,7 +230,7 @@
 
 def last_order(members, zs):
     teams = range(members // zs)
-    return [t * zs + z for z in range(zs)[::-1] for t in teams[::-1]]
+    return [t * zs + z for t in teams[::-1] for z in range(zs)[::-1]]
 
 
 def mix_kernel(share, spread_ref, own_ref, *refs):
@@ -314,7 +324,14 @@
         2 * zs,
         share,
     )
-    rows = lax.all_to_all(sent, COL, split_axis=0, concat_axis=0, tiled=True)
+    rows = lax.all_to_all(
+        sent,
+        COL,
+        split_axis=0,
+        concat_axis=0,
+        axis_index_groups=[ring_order(2 * zs)],
+        tiled=True,
+    )
 
     both, high, low = first_products(3, rows, factor, occ_cols, emp_cols, trial_vectors, share)
     held = (rows, factor, occ_cols, emp_cols, high, low, share)

time: 61.3 us -> 60.8 us (level)
  blocking collectives: 42.9 us -> 38.5 us
  waiting for transfers between devices: 2.35 us -> 5.93 us
    ppermute x1, starting transfers between devices: 3.58 us -> 0.01 us  [body(): from_both = lax.ppermute(both, ALL, pairs_of(teams, zs, 1, 1))]
    ppermute x1, waiting for transfers between devices: 0.01 us -> 3.52 us  [body(): lax.ppermute(second, ALL, pairs_of(teams, zs, 1 - (FIRST & 1), 1 - (FIRST...]
    all_to_all x1, blocking collectives: 20.5 us -> 17.6 us  [body(): lax.all_to_all(sent, COL, split_axis=0, concat_axis=0, axis_index_groups=...]
    ppermute x1, starting transfers between devices: 0.09 us -> 2.91 us  [body(): lax.ppermute(first, ALL, pairs_of(teams, zs, FIRST & 1, FIRST >> 1))]
    all_to_all x1, blocking collectives: 22.4 us -> 20.9 us  [body(): lax.all_to_all(sent, ('tm', 'zh'), split_axis=0, concat_axis=0, axis_inde...]
    ppermute x1, starting transfers between devices: 1.56 us -> 2.68 us  [body(): lax.ppermute(second, ALL, pairs_of(teams, zs, 1 - (FIRST & 1), 1 - (FIRST...]
  transfers between devices with their start and end apart: 3 -> 3, of which waited for: 1 -> 2; matrix products, arithmetic and copies ran while one was open for 0% -> 0% of each run, Pallas kernels for 7% -> 7%
where the time goes in v6:
time: 60.8 us; the launch traced here: 60.7 us
  blocking collectives  38.5 us (63%)
  Pallas kernels  10.5 us (17%)
  waiting for transfers between devices  5.93 us (10%)
  starting transfers between devices  5.59 us (9%)
    all_to_all x1, blocking collectives, body(): lax.all_to_all(sent, ('tm', 'zh'), split_axis=0, concat_axis=0, axis_inde...  20.9 us
    all_to_all x1, blocking collectives, body(): lax.all_to_all(sent, COL, split_axis=0, concat_axis=0, axis_index_groups=...  17.6 us
    pallas_call x3, Pallas kernels, next_products(): pl.pallas_call(functools.partial(table_kernel if grid else next_kernel, s...  6.16 us
    ppermute x1, waiting for transfers between devices, body(): lax.ppermute(second, ALL, pairs_of(teams, zs, 1 - (FIRST & 1), 1 - (FIRST...  3.52 us
    ppermute x1, starting transfers between devices, body(): lax.ppermute(first, ALL, pairs_of(teams, zs, FIRST & 1, FIRST >> 1))  2.91 us
    ppermute x1, starting transfers between devices, body(): lax.ppermute(second, ALL, pairs_of(teams, zs, 1 - (FIRST & 1), 1 - (FIRST...  2.68 us
    ppermute x1, waiting for transfers between devices, body(): from_both = lax.ppermute(both, ALL, pairs_of(teams, zs, 1, 1))  2.42 us
    pallas_call x1, Pallas kernels, first_products(): pl.pallas_call(functools.partial(first_kernel, share, part), out_shape=(j...  1.84 us
  transfers between devices with their start and end apart: 3, of which 2 were waited for; matrix products, arithmetic and copies ran while one was open for 0% of the time, Pallas kernels for 7%

profile of v6, /device:TPU:1, one launch (start us, length us, event | category | flops | bytes accessed | tf_op | source)
XLA Modules:
  0.0 60.7 jit_solution(2219258663363876180)
XLA Ops:
  0.0 0.0 copy-start
  0.0 0.0 copy-start.1
  0.0 0.0 copy-start.2
  0.0 1.4 %shard_map.100 = (bf16[16,8,1024]{2,1,0:T(8,128)(2,1)S(1)}, f32[2,16,1024]{2,1,0:T(8,128)S(1)}) custom-call(f32[1,16]{1,0:T(1,128)} %bitcast.5, f32[1,1024]{1,0:T(1,128)} %bitcast.8, f32[1,1024]{1,0:T(1,128)} %bitcast.9, bf16[64,1024]{1,0:T(8,128)(2,1)} %bitcast.6, bf16[64,1024]{1,0:T(8,128)(2,1)} %bitcast.7), custom_call_target="tpu_custom_call" | custom-call | flops 34359738368 | bytes 1048576 | tf_op jit(solution)/shard_map/pallas_call | solution.py:86
  1.4 17.6 %all_to_all.10.rows_ref.refs_0_ = bf16[16,8,1024]{2,1,0:T(8,128)(2,1)S(1)} all-to-all(bf16[16,8,1024]{2,1,0:T(8,128)(2,1)S(1)} %get-tuple-element.12), channel_id=1, replica_groups={{0,14,12,10,8,6,4,2,1,15,13,11,9,7,5,3},{16,30,28,26,24,22,20,18,17,31,..., dimensions={0} | all-to-all | bytes 524288 | tf_op jit(solution)/shard_map/all_to_all | solution.py:327
  19.0 0.0 copy-done
  19.0 0.0 copy-done.1
  19.0 0.0 copy-done.2
  19.0 1.8 %shard_map.101 = (bf16[256,512]{1,0:T(8,128)(2,1)S(1)}, bf16[1024,512]{1,0:T(8,128)(2,1)S(1)}, bf16[1024,512]{1,0:T(8,128)(2,1)S(1)}) custom-call(bf16[16,8,1024]{2,1,0:T(8,128)(2,1)S(1)} %all_to_all.10.rows_ref.refs_0_, f32[2,16,1024]{2,1,0:T(8,128)S(1)} %get-tuple-element.13.factor_ref.refs_1_, bf16[1024,1024]{1,0:T(8,128)(2,1)S(1)} %copy-done, ...), custom_call_target="tpu_custom_call" | custom-call | flops 1610612736 | bytes 8388608 | tf_op jit(solution)/shard_map/pallas_call | solution.py:199
  20.9 1.8 %shard_map.103 = bf16[256,512]{1,0:T(8,128)(2,1)S(1)} custom-call(bf16[16,8,1024]{2,1,0:T(8,128)(2,1)S(1)} %all_to_all.10.rows_ref.refs_0_, f32[2,16,1024]{2,1,0:T(8,128)S(1)} %get-tuple-element.13.factor_ref.refs_1_, bf16[1024,1024]{1,0:T(8,128)(2,1)S(1)} %copy-done, bf16[1024,1024]{1,0:T(8,128)(2,1)S(1)} %copy-done.1, ...), custom_call_target="tpu_custom_call" | custom-call | flops 1610612736 | bytes 8388608 | tf_op jit(solution)/shard_map/pallas_call | solution.py:220
  22.7 2.9 %collective-permute-start.1 = (bf16[256,512]{1,0:T(8,128)(2,1)S(1)}, bf16[256,512]{1,0:T(8,128)(2,1)S(1)}, u32[]{:S(2)}, u32[]{:S(2)}) collective-permute-start(bf16[256,512]{1,0:T(8,128)(2,1)S(1)} %shard_map.103), channel_id=1, source_target_pairs={{0,2},{1,3},{2,0},{3,1},{4,6},{5,7},{6,4},{7,5},{8,10},{9,11},{10,... | collective-permute-start | bytes 786440 | tf_op jit(solution)/shard_map/ppermute | solution.py:340
  25.6 1.8 %shard_map.104 = bf16[256,512]{1,0:T(8,128)(2,1)S(1)} custom-call(bf16[16,8,1024]{2,1,0:T(8,128)(2,1)S(1)} %all_to_all.10.rows_ref.refs_0_, f32[2,16,1024]{2,1,0:T(8,128)S(1)} %get-tuple-element.13.factor_ref.refs_1_, bf16[1024,1024]{1,0:T(8,128)(2,1)S(1)} %copy-done, bf16[1024,1024]{1,0:T(8,128)(2,1)S(1)} %copy-done.1, ...), custom_call_target="tpu_custom_call" | custom-call | flops 1610612736 | bytes 8388608 | tf_op jit(solution)/shard_map/pallas_call | solution.py:220
  27.4 2.7 %collective-permute-start.2 = (bf16[256,512]{1,0:T(8,128)(2,1)S(1)}, bf16[256,512]{1,0:T(8,128)(2,1)S(1)}, u32[]{:S(2)}, u32[]{:S(2)}) collective-permute-start(bf16[256,512]{1,0:T(8,128)(2,1)S(1)} %shard_map.104), channel_id=1, source_target_pairs={{0,1},{1,0},{2,3},{3,2},{4,5},{5,4},{6,7},{7,6},{8,9},{9,8},{10,11... | collective-permute-start | bytes 786440 | tf_op jit(solution)/shard_map/ppermute | solution.py:342
  30.0 0.0 collective-permute-start
  30.0 2.6 %shard_map.102 = (f32[256,512]{1,0:T(8,128)S(1)}, bf16[2,256,256]{2,1,0:T(8,128)(2,1)S(1)}) custom-call(f32[16]{0:T(128)} %times_ref.1, f32[16]{0:T(128)} %weights_ref.1, f32[16]{0:T(128)} %freqs_ref.1, bf16[16,8,1024]{2,1,0:T(8,128)(2,1)S(1)} %all_to_all.10.rows_ref.refs_0_, f32[2,16,1024]{2,1,0:T(8,128)S(1)} %get-tuple-element.13.factor_ref.refs_1_, ...), custom_call_target="tpu_custom_call" | custom-call | flops 1610612736 | bytes 8388608 | tf_op jit(solution)/shard_map/pallas_call | solution.py:220
  32.6 0.0 collective-permute-done.1.refs_1_
  32.7 3.5 %collective-permute-done.2.refs_2_ = bf16[256,512]{1,0:T(8,128)(2,1)S(1)} collective-permute-done((bf16[256,512]{1,0:T(8,128)(2,1)S(1)}, bf16[256,512]{1,0:T(8,128)(2,1)S(1)}, u32[]{:S(2)}, u32[]{:S(2)}) %collective-permute-start.2) | collective-permute-done | bytes 262176 | tf_op jit(solution)/shard_map/ppermute | solution.py:342
  36.2 2.4 %collective-permute-done.refs_0_ = bf16[256,512]{1,0:T(8,128)(2,1)S(1)} collective-permute-done((bf16[256,512]{1,0:T(8,128)(2,1)S(1)}, bf16[256,512]{1,0:T(8,128)(2,1)S(1)}, u32[]{:S(2)}, u32[]{:S(2)}) %collective-permute-start) | collective-permute-done | bytes 262176 | tf_op jit(solution)/shard_map/ppermute | solution.py:338
  38.6 0.4 shard_map.105
  39.0 20.9 %all_to_all.11.got_ref = bf16[64,4,512]{2,1,0:T(4,128)(2,1)S(1)} all-to-all(bf16[64,4,512]{2,1,0:T(4,128)(2,1)S(1)} %shard_map.105), channel_id=1, replica_groups={{252,248,244,240,236,232,228,224,220,216,212,208,204,200,196,192,188,18..., dimensions={0} | all-to-all | bytes 524288 | tf_op jit(solution)/shard_map/all_to_all | solution.py:346
  60.0 0.7 %shard_map.106 = f32[1,64,512]{2,1,0:T(8,128)} custom-call(bf16[64,4,512]{2,1,0:T(4,128)(2,1)S(1)} %all_to_all.11.got_ref), custom_call_target="tpu_custom_call" | custom-call | tf_op jit(solution)/shard_map/pallas_call | solution.py:280
Async XLA Ops:
  0.0 19.0 %copy-start = (bf16[1024,1024]{1,0:T(8,128)(2,1)S(1)}, bf16[1024,1024]{1,0:T(8,128)(2,1)}, u32[]{:S(2)}) copy-start(bf16[1024,1024]{1,0:T(8,128)(2,1)} %occ_ref.5) | copy-start | bytes 6291460
  0.0 19.0 %copy-start.1 = (bf16[1024,1024]{1,0:T(8,128)(2,1)S(1)}, bf16[1024,1024]{1,0:T(8,128)(2,1)}, u32[]{:S(2)}) copy-start(bf16[1024,1024]{1,0:T(8,128)(2,1)} %emp_ref.5) | copy-start | bytes 6291460
  0.0 19.0 %copy-start.2 = (f32[1024,512]{1,0:T(8,128)S(1)}, f32[1024,512]{1,0:T(8,128)}, u32[]{:S(2)}) copy-start(f32[1024,512]{1,0:T(8,128)} %trial_ref.1) | copy-start | bytes 6291460
  22.7 10.0 %collective-permute-start.1 = (bf16[256,512]{1,0:T(8,128)(2,1)S(1)}, bf16[256,512]{1,0:T(8,128)(2,1)S(1)}, u32[]{:S(2)}, u32[]{:S(2)}) collective-permute-start(bf16[256,512]{1,0:T(8,128)(2,1)S(1)} %shard_map.103), channel_id=1, source_target_pairs={{0,2},{1,3},{2,0},{3,1},{4,6},{5,7},{6,4},{7,5},{8,10},{9,11},{10,... | collective-permute-start | bytes 786440 | tf_op jit(solution)/shard_map/ppermute | solution.py:340
  27.4 8.8 %collective-permute-start.2 = (bf16[256,512]{1,0:T(8,128)(2,1)S(1)}, bf16[256,512]{1,0:T(8,128)(2,1)S(1)}, u32[]{:S(2)}, u32[]{:S(2)}) collective-permute-start(bf16[256,512]{1,0:T(8,128)(2,1)S(1)} %shard_map.104), channel_id=1, source_target_pairs={{0,1},{1,0},{2,3},{3,2},{4,5},{5,4},{6,7},{7,6},{8,9},{9,8},{10,11... | collective-permute-start | bytes 786440 | tf_op jit(solution)/shard_map/ppermute | solution.py:342
  30.0 8.5 %collective-permute-start = (bf16[256,512]{1,0:T(8,128)(2,1)S(1)}, bf16[256,512]{1,0:T(8,128)(2,1)S(1)}, u32[]{:S(2)}, u32[]{:S(2)}) collective-permute-start(bf16[256,512]{1,0:T(8,128)(2,1)S(1)} %get-tuple-element.18), channel_id=1, source_target_pairs={{0,3},{1,2},{2,1},{3,0},{4,7},{5,6},{6,5},{7,4},{8,11},{9,10},{10,... | collective-permute-start | bytes 786440 | tf_op jit(solution)/shard_map/ppermute | solution.py:338
